TPU v7x, 32 devices: a whole 2x2x4 slice. The times are simulated.
32 devices in a mesh: row: 2 (over x), col: 4 (over y, core), layer: 4 (over z).
Axes of the slice: x: 2, y: 2, z: 4, core: 2. Of those that a mesh axis runs over, the one named last changes fastest.
Arguments:
- flow_matrix: float32 [2048, 2048], P('row', ('layer', 'col')), may hold values from 0.0009 to 310, as said below
- regularizer: float32 [2048, 2048], P(('layer', 'row'), 'col'), may hold values from 0.001 to 1
- pattern: int32 [8, 8], replicated, may hold values from 0 to 1, as said below
Outputs:
- inflated: float32 [2048, 2048], P(('row', 'layer'), 'col')
Inputs may be any that keep to these rules, and one draw needn't show every extreme that they name: `flow_matrix`: entries are positive. `pattern`: each entry is 0 or 1; every diagonal entry is 1.
All inputs are finite; a program needn't handle non-finite values.
Results may differ from a plain program's by a relative error of at most 0.000098.
Values sent between devices are 32-bit elements; how exact they have to be, the bound alone decides.
No kernel may reach another device: no remote copies, remote signals or barrier semaphores. Data moves between devices by JAX's collectives and lax.ppermute only.
A program may use at most 64 MiB of HBM per device.

v0:
```python
import jax
import jax.numpy as jnp
from jax import lax
from jax.sharding import PartitionSpec as P

TILE = 256


def keep_tiles(values, pattern, row_start, col_start):
    tile_count = pattern.shape[0]
    row_tile = (row_start + lax.iota(jnp.int32, values.shape[0])) // TILE
    col_tile = (col_start + lax.iota(jnp.int32, values.shape[1])) // TILE
    tile_ids = lax.iota(jnp.int32, tile_count)
    row_pick = (row_tile[:, None] == tile_ids[None, :]).astype(jnp.float32)
    col_pick = (col_tile[:, None] == tile_ids[None, :]).astype(jnp.float32)
    pattern_rows = jnp.dot(
        row_pick,
        pattern.astype(jnp.float32),
        precision=lax.Precision.HIGHEST,
        preferred_element_type=jnp.float32,
    )
    chosen = jnp.dot(
        pattern_rows,
        col_pick.T,
        precision=lax.Precision.HIGHEST,
        preferred_element_type=jnp.float32,
    )
    return values * chosen


def shards(flow_matrix, regularizer, pattern):
    order_total = flow_matrix.shape[0] * lax.axis_size("row")
    left_whole = lax.all_gather(flow_matrix, "col", axis=1, tiled=True)
    partial_value = jnp.dot(
        left_whole,
        lax.all_gather(regularizer, "row", axis=0, tiled=True),
        precision=lax.Precision.HIGHEST,
        preferred_element_type=jnp.float32,
    )
    own_count = partial_value.shape[0] // lax.axis_size("layer")
    col_start = lax.axis_index("col") * partial_value.shape[1]
    expanded = lax.psum_scatter(partial_value, "layer", scatter_dimension=0, tiled=True)
    row_start = lax.axis_index("row") * partial_value.shape[0] + lax.axis_index("layer") * own_count
    pruned = keep_tiles(expanded, pattern, row_start, col_start)
    squared = pruned * pruned
    totals = lax.psum(jnp.sum(squared, axis=0), ("row", "layer"))
    inflated = squared / totals[None, :] * order_total
    return inflated


def solution(mesh):
    return jax.shard_map(
        shards,
        mesh=mesh,
        in_specs=(P("row", ("layer", "col")), P(("layer", "row"), "col"), P()),
        out_specs=P(("row", "layer"), "col"),
        check_vma=False,
    )
```

profile of v0, /device:TPU:0, one launch (start us, length us, event | category | flops | bytes accessed | tf_op | source)
XLA Modules:
  0.0 136.4 jit_solution(12964221598717887879)
XLA Ops:
  6.5 0.0 all-gather.5.cloned.1.call-start
  6.5 0.7 all-gather.5.cloned.1.call-update
  7.3 0.0 all-gather.3.cloned.1.call-start
  7.3 0.7 all-gather.3.cloned.1.call-update
  8.0 0.0 reduce-scatter.2.cloned.1.call-start
  8.1 24.9 %all-gather.5.cloned.1.call-done = f32[512,512]{1,0:T(8,128)} async-done(((f32[256,512]{1,0:T(8,128)}), f32[512,512]{1,0:T(8,128)}) %all-gather.5.cloned.1.call-update) | async-done | bytes 1048592 | tf_op jit(solution)/shard_map/all_gather | solution.py:36
  32.9 24.4 %all-gather.3.cloned.1.call-done = f32[1024,512]{1,0:T(8,128)} async-done(((f32[1024,128]{1,0:T(8,128)}), f32[1024,512]{1,0:T(8,128)}) %all-gather.3.cloned.1.call-update) | async-done | bytes 2097168 | tf_op jit(solution)/shard_map/all_gather | solution.py:33
  57.3 6.6 %fusion.9 = f32[1024,512]{1,0:T(8,128)} fusion(f32[1024,512]{1,0:T(8,128)} %all-gather.3.cloned.1.call-done, f32[512,512]{1,0:T(8,128)} %all-gather.5.cloned.1.call-done), kind=kOutput, calls=%fused_computation.23 | convolution fusion | flops 3221225472 | bytes 5242880 | tf_op jit(solution)/shard_map/dot_general | solution.py:34
  63.9 0.0 copy-start
  63.9 0.0 reduce-scatter.2.cloned.1.call-update
  64.0 0.6 copy-done
  64.6 0.3 fusion.2
  64.9 42.9 %reduce-scatter.2.cloned.1.call-done = f32[256,512]{1,0:T(8,128)} async-done(((f32[1024,512]{1,0:T(8,128)}), f32[256,512]{1,0:T(8,128)}) %reduce-scatter.2.cloned.1.call-update) | async-done | bytes 524304 | tf_op jit(solution)/shard_map/reduce_scatter | solution.py:42
  107.8 1.6 %fusion.8 = (f32[512]{0:T(512)S(1)}, f32[256,512]{1,0:T(8,128)S(1)}) fusion(f32[256,512]{1,0:T(8,128)} %reduce-scatter.2.cloned.1.call-done, f32[256,8]{1,0:T(8,128)S(1)} %fusion.2, s32[512]{0:T(512)S(1)} %add_select_fusion), kind=kOutput, calls=%fused_computation.22 | convolution fusion | flops 12979712 | bytes 1060864 | tf_op jit(solution)/shard_map/dot_general | solution.py:22
  109.3 19.7 %psum.7 = f32[512]{0:T(512)S(1)} all-reduce(f32[512]{0:T(512)S(1)} %get-tuple-element.5), channel_id=1, replica_groups=mesh['row'=2,'col'=4,'layer'=4] {'row','layer'}, use_global_device_ids=true, to_apply=%region_2.3 | all-reduce | flops 512 | bytes 4096 | tf_op jit(solution)/shard_map/psum | solution.py:46
  129.0 0.9 divide_multiply_fusion
  (2 shorter events, 0.0 us)
Async XLA Ops:
  6.5 26.4 %all-gather.5.cloned.1.call-start = ((), (), s32[]{:S(2)}) async-start(), calls=%async_computation.2 | async-start | bytes 1572864 | tf_op jit(solution)/shard_map/all_gather | solution.py:36
  7.3 50.1 %all-gather.3.cloned.1.call-start = ((), (), s32[]{:S(2)}) async-start(), calls=%async_computation.1 | async-start | bytes 2621440 | tf_op jit(solution)/shard_map/all_gather | solution.py:33
  8.0 99.8 %reduce-scatter.2.cloned.1.call-start = ((), (), s32[]{:S(2)}) async-start(), calls=%async_computation.3 | async-start | bytes 2621440 | tf_op jit(solution)/shard_map/reduce_scatter | solution.py:42
  63.9 0.7 copy-start
Sparse Core Ops, SparseCore 0:
  8.9 23.9 all-gather.4
  34.5 22.8 all-gather.2
  64.1 43.6 reduce-scatter.1
where the time goes:
time: 137 us; the launch traced here: 136 us
  waiting for transfers between devices  93.5 us (68%)
  blocking collectives  19.7 us (14%)
  between operations  13.1 us (10%)
  matrix products  8.44 us (6%)
    reduce_scatter x1, waiting for transfers between devices, shards(): lax.psum_scatter(partial_value, 'layer', scatter_dimension=0, tiled=True)  42.9 us
    all_gather x1, waiting for transfers between devices, shards(): lax.all_gather(regularizer, 'row', axis=0, tiled=True)  24.9 us
    all_gather x1, waiting for transfers between devices, shards(): left_whole = lax.all_gather(flow_matrix, 'col', axis=1, tiled=True)  24.4 us
    psum x1, blocking collectives, shards(): totals = lax.psum(jnp.sum(squared, axis=0), ('row', 'layer'))  19.7 us
    dot_general x1, matrix products, shards(): jnp.dot(left_whole, lax.all_gather(regularizer, 'row', axis=0, tiled=True...  6.63 us
  transfers between devices with their start and end apart: 3, of which 3 were waited for; matrix products, arithmetic and copies ran while one was open for 0% of the time, Pallas kernels for 0%

commit v1 on v0

v1 whole, which is shorter than its diff:
```python
import jax
import jax.numpy as jnp
from jax import lax
from jax.sharding import PartitionSpec as P


def bits_of(count):
    bits, bit = [], 1
    while bit < count:
        bits.append(bit)
        bit *= 2
    return bits[::-1]


def swap(value, axis, bit):
    return lax.ppermute(value, axis, [(i, i ^ bit) for i in range(lax.axis_size(axis))])


def far_pieces(value, axis, skip):
    pieces = {0: value}
    for bit in bits_of(lax.axis_size(axis)):
        if bit > skip:
            for j in list(pieces):
                pieces[j ^ bit] = swap(pieces[j], axis, bit)
    del pieces[0]
    return pieces


def in_order(pieces, axis, dim):
    index = lax.axis_index(axis)
    blocks = [pieces[j] for j in range(len(pieces))]
    for bit in bits_of(len(pieces)):
        flip = (index & bit) != 0
        blocks = [jnp.where(flip, blocks[j ^ bit], blocks[j]) for j in range(len(blocks))]
    return jnp.concatenate(blocks, axis=dim)


def total_over(value, axis):
    for bit in bits_of(lax.axis_size(axis))[::-1]:
        value = value + swap(value, axis, bit)
    return value


def kept_tiles(pattern, row_start, row_count, col_start, col_count, tile):
    ids = lax.iota(jnp.int32, pattern.shape[0])
    row_tile = (row_start + lax.iota(jnp.int32, row_count)) // tile
    col_tile = (col_start + lax.iota(jnp.int32, col_count)) // tile
    row_pick = (row_tile[:, None] == ids[None, :]).astype(jnp.float32)
    col_pick = (ids[:, None] == col_tile[None, :]).astype(jnp.float32)
    return jnp.dot(jnp.dot(row_pick, pattern.astype(jnp.float32)), col_pick)


def exchange(value, targets):
    return lax.ppermute(value, "layer", list(enumerate(targets)))


def shards(flow_matrix, regularizer, pattern):
    row_count, layer_count = lax.axis_size("row"), lax.axis_size("layer")
    order_total = flow_matrix.shape[0] * row_count
    tile = order_total // pattern.shape[0]
    rows, width = flow_matrix.shape[0], regularizer.shape[1]
    own, part = rows // layer_count, width // 2
    row, col, layer = (lax.axis_index(a) for a in ("row", "col", "layer"))
    last = layer_count - 1
    end = (layer == 0) | (layer == last)

    def blocks_of(values, offsets):
        blocks = [lax.dynamic_slice_in_dim(values, (layer ^ k) * own, own, 0) for k in offsets]
        return jnp.concatenate(blocks, axis=0)

    near = swap(flow_matrix, "col", 1)

    def gather_left(offsets):
        mine = blocks_of(flow_matrix, offsets)
        pieces = far_pieces(mine, "col", 1)
        for j in list(pieces):
            pieces[j ^ 1] = swap(pieces[j], "col", 1)
        pieces.update({0: mine, 1: blocks_of(lax.optimization_barrier(near), offsets)})
        return in_order(lax.optimization_barrier(pieces), "col", 1)

    def gather_right(value):
        pieces = far_pieces(value, "row", 0)
        pieces[0] = value
        return in_order(pieces, "row", 0)

    first = gather_left((2, 3))
    rest = gather_left((1, 0))
    rights = [gather_right(lax.optimization_barrier(regularizer[:, h * part:(h + 1) * part])) for h in range(2)]

    def product(left, right):
        value = jnp.dot(
            left, right, precision=lax.Precision.HIGH, preferred_element_type=jnp.float32
        )
        return lax.optimization_barrier(value)

    kept = kept_tiles(pattern, row * rows + layer * own, own, col * width, width, tile)
    relay = (1, last, 0, last - 1)
    right = jnp.concatenate(rights, axis=1)
    seconds = [exchange(product(first[:own], rights[h]), relay) for h in range(2)]
    third = product(first[own:], right)
    across = lax.ppermute(third, "layer", [(0, last), (last, 0)])
    others = product(rest, right)
    beside = swap(others[:own], "layer", 1)
    seconds = jnp.concatenate(seconds, axis=1)
    passed = lax.ppermute(third + seconds, "layer", [(1, 2), (2, 1)])
    expanded = others[own:] + beside + across + passed + jnp.where(end, seconds, 0.0)
    pruned = expanded * kept
    squared = pruned * pruned
    totals = jnp.sum(squared, axis=0, keepdims=True)
    totals = total_over(total_over(totals, "row"), "layer")
    return squared / totals * order_total


def solution(mesh):
    return jax.shard_map(
        shards,
        mesh=mesh,
        in_specs=(P("row", ("layer", "col")), P(("layer", "row"), "col"), P()),
        out_specs=P(("row", "layer"), "col"),
        check_vma=False,
    )
```

time: 137 us -> 73.7 us (0.54)
  waiting for transfers between devices: 93.5 us -> 40.2 us
  starting transfers between devices: 0.08 us -> 23.8 us
  blocking collectives: 19.7 us -> 0 us
  between operations: 13.1 us -> 0.22 us
  matrix products: 8.44 us -> 2.84 us
  other arithmetic: 0.89 us -> 3.65 us
  local copies, waits for them, and re-layouts: 0.62 us -> 2.76 us
    all_gather x2 -> x0, waiting for transfers between devices: 49.3 us -> none  [the longest x1 24.9 us: shards(): lax.all_gather(regularizer, 'row', axis=0, tiled=True)]
    reduce_scatter x1 -> x0, waiting for transfers between devices: 42.9 us -> none  [shards(): lax.psum_scatter(partial_value, 'layer', scatter_dimension=0, tiled=True)]
    ppermute x0 -> x15, waiting for transfers between devices: none -> 40.2 us  [the longest x11 24 us: swap(): lax.ppermute(value, axis, [(i, i ^ bit) for i in range(lax.axis_size(axis...]
    ppermute x0 -> x15, starting transfers between devices: none -> 23.8 us  [the longest x11 14.6 us: swap(): lax.ppermute(value, axis, [(i, i ^ bit) for i in range(lax.axis_size(axis...]
    psum x1 -> x0, blocking collectives: 19.7 us -> none  [shards(): totals = lax.psum(jnp.sum(squared, axis=0), ('row', 'layer'))]
    dot_general x3 -> x5, matrix products: 8.44 us -> 2.84 us  [the longest x4 2.47 us: product(): jnp.dot(left, right, precision=lax.Precision.HIGH, preferred_element_type...]
    reduce_sum x0 -> x1, other arithmetic: none -> 1.46 us  [shards(): totals = jnp.sum(squared, axis=0, keepdims=True)]
    unnamed x3 -> x0, waiting for transfers between devices: 1.42 us -> none
  transfers between devices with their start and end apart: 3 -> 15, of which waited for: 3 -> 9; matrix products, arithmetic and copies ran while one was open for 0% -> 6% of each run, Pallas kernels for 0% -> 0%
where the time goes in v1:
time: 73.7 us; the launch traced here: 73.5 us
  waiting for transfers between devices  40.2 us (55%)
  starting transfers between devices  23.8 us (32%)
  other arithmetic  3.65 us (5%)
  matrix products  2.84 us (4%)
  local copies, waits for them, and re-layouts  2.76 us (4%)
    ppermute x11, waiting for transfers between devices, swap(): lax.ppermute(value, axis, [(i, i ^ bit) for i in range(lax.axis_size(axis...  24 us
    ppermute x11, starting transfers between devices, swap(): lax.ppermute(value, axis, [(i, i ^ bit) for i in range(lax.axis_size(axis...  14.6 us
    ppermute x1, waiting for transfers between devices, shards(): across = lax.ppermute(third, 'layer', [(0, last), (last, 0)])  12.6 us
    ppermute x2, starting transfers between devices, exchange(): return lax.ppermute(value, 'layer', list(enumerate(targets)))  4.47 us
    ppermute x2, waiting for transfers between devices, exchange(): return lax.ppermute(value, 'layer', list(enumerate(targets)))  3.63 us
    ppermute x1, starting transfers between devices, shards(): across = lax.ppermute(third, 'layer', [(0, last), (last, 0)])  3.24 us
    dot_general x4, matrix products, product(): jnp.dot(left, right, precision=lax.Precision.HIGH, preferred_element_type...  2.47 us
  transfers between devices with their start and end apart: 15, of which 9 were waited for; matrix products, arithmetic and copies ran while one was open for 6% of the time, Pallas kernels for 0%

profile of v1, /device:TPU:0, one launch (start us, length us, event | category | flops | bytes accessed | tf_op | source)
XLA Modules:
  0.0 73.5 jit_solution(4749805924836993869)
XLA Ops:
  0.0 1.1 %constant_dynamic-slice_fusion.7 = (f32[256,128]{1,0:T(8,128)S(1)}, f32[256,128]{1,0:T(8,128)S(1)}, f32[256,128]{1,0:T(8,128)S(1)}, f32[256,128]{1,0:T(8,128)S(1)}) fusion(f32[1024,128]{1,0:T(8,128)} %param.3, s32[]{:T(128)S(6)} %select_n.134, s32[]{:T(128)S(6)} %select_n.135, s32[]{:T(128)S(6)} %select_n.150, s32[]{:T(128)S(6)} %select_n.149), kind=kLoop, calls=%fused_computation.77 | loop fusion | bytes 1048592 | tf_op jit(solution)/shard_map/dynamic_slice | solution.py:68
  1.2 3.1 %collective-permute-start.6 = (f32[512,128]{1,0:T(8,128)S(1)}, f32[512,128]{1,0:T(8,128)S(1)}, u32[]{:S(2)}, u32[]{:S(2)}) collective-permute-start(f32[512,128]{1,0:T(8,128)S(1)} %pad_maximum_fusion.3), channel_id=1, source_target_pairs={{0,8},{4,12},{8,0},{12,4},{1,9},{5,13},{9,1},{13,5},{2,10},{6,14},... | collective-permute-start | bytes 786440 | tf_op jit(solution)/shard_map/ppermute | solution.py:16
  4.4 2.0 %collective-permute-start.3 = (f32[256,256]{1,0:T(8,128)S(1)}, f32[256,256]{1,0:T(8,128)S(1)}, u32[]{:S(2)}, u32[]{:S(2)}) collective-permute-start(f32[256,256]{1,0:T(8,128)S(1)} %get-tuple-element.42), channel_id=1, source_target_pairs={{0,16},{16,0},{1,17},{17,1},{2,18},{18,2},{3,19},{19,3},{4,20},{20... | collective-permute-start | bytes 786440 | tf_op jit(solution)/shard_map/ppermute | solution.py:16
  6.4 0.4 collective-permute-start.4
  6.8 4.6 %collective-permute-done.6 = f32[512,128]{1,0:T(8,128)S(1)} collective-permute-done((f32[512,128]{1,0:T(8,128)S(1)}, f32[512,128]{1,0:T(8,128)S(1)}, u32[]{:S(2)}, u32[]{:S(2)}) %collective-permute-start.6) | collective-permute-done | bytes 262176 | tf_op jit(solution)/shard_map/ppermute | solution.py:16
  11.4 4.8 %collective-permute-done.1 = f32[512,128]{1,0:T(8,128)S(1)} collective-permute-done((f32[512,128]{1,0:T(8,128)S(1)}, f32[512,128]{1,0:T(8,128)S(1)}, u32[]{:S(2)}, u32[]{:S(2)}) %collective-permute-start.1) | collective-permute-done | bytes 262176 | tf_op jit(solution)/shard_map/ppermute | solution.py:16
  16.2 1.6 %collective-permute-done.4 = f32[256,256]{1,0:T(8,128)S(1)} collective-permute-done((f32[256,256]{1,0:T(8,128)S(1)}, f32[256,256]{1,0:T(8,128)S(1)}, u32[]{:S(2)}, u32[]{:S(2)}) %collective-permute-start.4) | collective-permute-done | bytes 262176 | tf_op jit(solution)/shard_map/ppermute | solution.py:16
  18.0 0.1 broadcast_select_fusion.15
  18.2 0.4 fusion.18
  18.6 1.8 %collective-permute-start.9 = (f32[256,256]{1,0:T(8,128)S(1)}, f32[256,256]{1,0:T(8,128)S(1)}, u32[]{:S(2)}, u32[]{:S(2)}) collective-permute-start(f32[256,256]{1,0:T(8,128)S(1)} %fusion.18), channel_id=1, source_target_pairs={{0,1},{1,3},{2,0},{3,2},{4,5},{5,7},{6,4},{7,6},{8,9},{9,11},{10,8... | collective-permute-start | bytes 786440 | tf_op jit(solution)/shard_map/ppermute | solution.py:54
  20.4 0.4 fusion.22
  20.9 1.0 %fusion.3 = f32[512,512]{1,0:T(8,128)S(1)} fusion(f32[512,128]{1,0:T(8,128)S(1)} %get-tuple-element.26, f32[512,128]{1,0:T(8,128)S(1)} %get-tuple-element.25, f32[512,128]{1,0:T(8,128)S(1)} %get-tuple-element.24, f32[512,128]{1,0:T(8,128)S(1)} %get-tuple-element.23, f32[256,256]{1,0:T(8,128)S(1)} %get-tuple-element.40, ...), kind=kOutput, calls=%fused_computation.2 | convolution fusion | flops 806879232 | bytes 3145728 | tf_op jit(solution)/shard_map/dot_general | solution.py:91
  22.0 2.6 %collective-permute-start.10 = (f32[256,256]{1,0:T(8,128)S(1)}, f32[256,256]{1,0:T(8,128)S(1)}, u32[]{:S(2)}, u32[]{:S(2)}) collective-permute-start(f32[256,256]{1,0:T(8,128)S(1)} %fusion.22), channel_id=1, source_target_pairs={{0,1},{1,3},{2,0},{3,2},{4,5},{5,7},{6,4},{7,6},{8,9},{9,11},{10,8... | collective-permute-start | bytes 786440 | tf_op jit(solution)/shard_map/ppermute | solution.py:54
  24.6 0.6 fusion.11
  25.3 0.8 %slice.26 = f32[256,512]{1,0:T(8,128)} slice(f32[512,512]{1,0:T(8,128)S(1)} %fusion.3), slice={[0:256], [0:512]} | slice | bytes 1048576 | tf_op jit(solution)/shard_map/slice | solution.py:103
  26.1 0.5 collective-permute-start.5
  26.6 3.2 %collective-permute-start.8 = (f32[256,512]{1,0:T(8,128)S(1)}, f32[256,512]{1,0:T(8,128)}, u32[]{:S(2)}, u32[]{:S(2)}) collective-permute-start(f32[256,512]{1,0:T(8,128)S(1)} %fusion.11), channel_id=1, source_target_pairs={{0,3},{3,0},{4,7},{7,4},{8,11},{11,8},{12,15},{15,12},{16,19},{19,... | collective-permute-start | bytes 1572872 | tf_op jit(solution)/shard_map/ppermute | solution.py:101
  29.9 3.6 %collective-permute-done.10 = f32[256,256]{1,0:T(8,128)S(1)} collective-permute-done((f32[256,256]{1,0:T(8,128)S(1)}, f32[256,256]{1,0:T(8,128)S(1)}, u32[]{:S(2)}, u32[]{:S(2)}) %collective-permute-start.10) | collective-permute-done | bytes 262176 | tf_op jit(solution)/shard_map/ppermute | solution.py:54
  33.5 0.9 %add.79 = f32[256,512]{1,0:T(8,128)} add(f32[256,512]{1,0:T(8,128)S(1)} %fusion.11, f32[256,512]{1,0:T(8,128)S(1)} %constant_dynamic-update-slice_fusion) | non-fusion elementwise | flops 131072 | bytes 1572864 | tf_op jit(solution)/shard_map/add | solution.py:105
  34.4 1.5 %collective-permute-start.11 = (f32[256,512]{1,0:T(8,128)}, f32[256,512]{1,0:T(8,128)}, u32[]{:S(2)}, u32[]{:S(2)}) collective-permute-start(f32[256,512]{1,0:T(8,128)} %add.79), channel_id=1, source_target_pairs={{1,2},{2,1},{5,6},{6,5},{9,10},{10,9},{13,14},{14,13},{17,18},{18,... | collective-permute-start | bytes 1572872 | tf_op jit(solution)/shard_map/ppermute | solution.py:105
  35.9 0.7 copy-done.2
  36.5 0.4 fusion
  36.9 7.7 %collective-permute-done.5 = f32[256,512]{1,0:T(8,128)S(1)} collective-permute-done((f32[256,512]{1,0:T(8,128)}, f32[256,512]{1,0:T(8,128)S(1)}, u32[]{:S(2)}, u32[]{:S(2)}) %collective-permute-start.5) | collective-permute-done | bytes 524320 | tf_op jit(solution)/shard_map/ppermute | solution.py:16
  44.6 12.6 %collective-permute-done.8 = f32[256,512]{1,0:T(8,128)} collective-permute-done((f32[256,512]{1,0:T(8,128)S(1)}, f32[256,512]{1,0:T(8,128)}, u32[]{:S(2)}, u32[]{:S(2)}) %collective-permute-start.8) | collective-permute-done | bytes 524320 | tf_op jit(solution)/shard_map/ppermute | solution.py:101
  57.3 1.5 %fusion.40 = (f32[512]{0:T(512)S(1)}, f32[256,512]{1,0:T(8,128)S(1)}) fusion(f32[256,512]{1,0:T(8,128)S(1)} %fusion, f32[256,512]{1,0:T(8,128)S(1)} %constant_dynamic-update-slice_fusion, pred[]{:T(512)S(6)} %or.3, f32[256,512]{1,0:T(8,128)} %collective-permute-done.11, f32[256,512]{1,0:T(8,128)} %collective-permute-done.8, ...), kind=kLoop, calls=%fused_computation.87 | loop fusion | flops 1048064 | bytes 3672065 | tf_op jit(solution)/shard_map/reduce_sum | solution.py:109
  58.7 1.5 %collective-permute-start.12 = (f32[1,512]{1,0:T(1,128)S(1)}, f32[1,512]{1,0:T(1,128)S(1)}, u32[]{:S(2)}, u32[]{:S(2)}) collective-permute-start(f32[1,512]{1,0:T(1,128)S(1)} %bitcast.2), channel_id=1, source_target_pairs={{0,16},{16,0},{1,17},{17,1},{2,18},{18,2},{3,19},{19,3},{4,20},{20... | collective-permute-start | bytes 6152 | tf_op jit(solution)/shard_map/ppermute | solution.py:16
  60.3 2.1 %collective-permute-done.12 = f32[1,512]{1,0:T(1,128)S(1)} collective-permute-done((f32[1,512]{1,0:T(1,128)S(1)}, f32[1,512]{1,0:T(1,128)S(1)}, u32[]{:S(2)}, u32[]{:S(2)}) %collective-permute-start.12) | collective-permute-done | bytes 2080 | tf_op jit(solution)/shard_map/ppermute | solution.py:16
  62.4 4.2 %collective-permute-start.13 = (f32[1,512]{1,0:T(1,128)S(1)}, f32[1,512]{1,0:T(1,128)S(1)}, u32[]{:S(2)}, u32[]{:S(2)}) collective-permute-start(f32[1,512]{1,0:T(1,128)S(1)} %add.87), channel_id=1, source_target_pairs={{0,1},{1,0},{2,3},{3,2},{4,5},{5,4},{6,7},{7,6},{8,9},{9,8},{10,11... | collective-permute-start | bytes 6152 | tf_op jit(solution)/shard_map/ppermute | solution.py:16
  66.5 1.6 %collective-permute-done.13 = f32[1,512]{1,0:T(1,128)S(1)} collective-permute-done((f32[1,512]{1,0:T(1,128)S(1)}, f32[1,512]{1,0:T(1,128)S(1)}, u32[]{:S(2)}, u32[]{:S(2)}) %collective-permute-start.13) | collective-permute-done | bytes 2080 | tf_op jit(solution)/shard_map/ppermute | solution.py:16
  68.1 2.9 %collective-permute-start.14 = (f32[1,512]{1,0:T(1,128)S(1)}, f32[1,512]{1,0:T(1,128)S(1)}, u32[]{:S(2)}, u32[]{:S(2)}) collective-permute-start(f32[1,512]{1,0:T(1,128)S(1)} %add.88), channel_id=1, source_target_pairs={{0,2},{1,3},{2,0},{3,1},{4,6},{5,7},{6,4},{7,5},{8,10},{9,11},{10,... | collective-permute-start | bytes 6152 | tf_op jit(solution)/shard_map/ppermute | solution.py:16
  71.0 1.6 %collective-permute-done.14 = f32[1,512]{1,0:T(1,128)S(1)} collective-permute-done((f32[1,512]{1,0:T(1,128)S(1)}, f32[1,512]{1,0:T(1,128)S(1)}, u32[]{:S(2)}, u32[]{:S(2)}) %collective-permute-start.14) | collective-permute-done | bytes 2080 | tf_op jit(solution)/shard_map/ppermute | solution.py:16
  72.6 0.9 %divide_multiply_fusion = f32[256,512]{1,0:T(8,128)} fusion(f32[256,512]{1,0:T(8,128)S(1)} %get-tuple-element.22, f32[512]{0:T(512)S(1)} %bitcast.4), kind=kLoop, calls=%fused_computation.28 | loop fusion | flops 262144 | bytes 1050624 | tf_op jit(solution)/shard_map/mul | solution.py:111
  (32 shorter events, 0.6 us)
Async XLA Ops:
  1.1 3.2 %copy-start = (f32[256,512]{1,0:T(8,128)S(1)}, f32[256,512]{1,0:T(8,128)}, u32[]{:S(2)}) copy-start(f32[256,512]{1,0:T(8,128)} %param.4) | copy-start | bytes 1572868
  1.2 10.2 %collective-permute-start.6 = (f32[512,128]{1,0:T(8,128)S(1)}, f32[512,128]{1,0:T(8,128)S(1)}, u32[]{:S(2)}, u32[]{:S(2)}) collective-permute-start(f32[512,128]{1,0:T(8,128)S(1)} %pad_maximum_fusion.3), channel_id=1, source_target_pairs={{0,8},{4,12},{8,0},{12,4},{1,9},{5,13},{9,1},{13,5},{2,10},{6,14},... | collective-permute-start | bytes 786440 | tf_op jit(solution)/shard_map/ppermute | solution.py:16
  4.3 2.2 %copy-start.1 = (f32[1024,128]{1,0:T(8,128)S(1)}, f32[1024,128]{1,0:T(8,128)}, u32[]{:S(2)}) copy-start(f32[1024,128]{1,0:T(8,128)} %param.3) | copy-start | bytes 1572868
  4.3 11.9 %collective-permute-start.1 = (f32[512,128]{1,0:T(8,128)S(1)}, f32[512,128]{1,0:T(8,128)S(1)}, u32[]{:S(2)}, u32[]{:S(2)}) collective-permute-start(f32[512,128]{1,0:T(8,128)S(1)} %pad_maximum_fusion.1), channel_id=1, source_target_pairs={{0,8},{4,12},{8,0},{12,4},{1,9},{5,13},{9,1},{13,5},{2,10},{6,14},... | collective-permute-start | bytes 786440 | tf_op jit(solution)/shard_map/ppermute | solution.py:16
  4.4 11.8 %collective-permute-start.3 = (f32[256,256]{1,0:T(8,128)S(1)}, f32[256,256]{1,0:T(8,128)S(1)}, u32[]{:S(2)}, u32[]{:S(2)}) collective-permute-start(f32[256,256]{1,0:T(8,128)S(1)} %get-tuple-element.42), channel_id=1, source_target_pairs={{0,16},{16,0},{1,17},{17,1},{2,18},{18,2},{3,19},{19,3},{4,20},{20... | collective-permute-start | bytes 786440 | tf_op jit(solution)/shard_map/ppermute | solution.py:16
  6.4 11.5 %collective-permute-start = (f32[1024,128]{1,0:T(8,128)S(1)}, f32[1024,128]{1,0:T(8,128)S(1)}, u32[]{:S(2)}, u32[]{:S(2)}) collective-permute-start(f32[1024,128]{1,0:T(8,128)S(1)} %copy-done.1), channel_id=1, source_target_pairs={{0,4},{4,0},{8,12},{12,8},{1,5},{5,1},{9,13},{13,9},{2,6},{6,2},{1... | collective-permute-start | bytes 1572872 | tf_op jit(solution)/shard_map/ppermute | solution.py:16
  6.4 11.4 %collective-permute-start.4 = (f32[256,256]{1,0:T(8,128)S(1)}, f32[256,256]{1,0:T(8,128)S(1)}, u32[]{:S(2)}, u32[]{:S(2)}) collective-permute-start(f32[256,256]{1,0:T(8,128)S(1)} %get-tuple-element.41), channel_id=1, source_target_pairs={{0,16},{16,0},{1,17},{17,1},{2,18},{18,2},{3,19},{19,3},{4,20},{20... | collective-permute-start | bytes 786440 | tf_op jit(solution)/shard_map/ppermute | solution.py:16
  11.4 6.6 %collective-permute-start.7 = (f32[512,128]{1,0:T(8,128)S(1)}, f32[512,128]{1,0:T(8,128)S(1)}, u32[]{:S(2)}, u32[]{:S(2)}) collective-permute-start(f32[512,128]{1,0:T(8,128)S(1)} %collective-permute-done.6), channel_id=1, source_target_pairs={{0,4},{4,0},{8,12},{12,8},{1,5},{5,1},{9,13},{13,9},{2,6},{6,2},{1... | collective-permute-start | bytes 786440 | tf_op jit(solution)/shard_map/ppermute | solution.py:16
  16.2 1.8 %collective-permute-start.2 = (f32[512,128]{1,0:T(8,128)S(1)}, f32[512,128]{1,0:T(8,128)S(1)}, u32[]{:S(2)}, u32[]{:S(2)}) collective-permute-start(f32[512,128]{1,0:T(8,128)S(1)} %collective-permute-done.1), channel_id=1, source_target_pairs={{0,4},{4,0},{8,12},{12,8},{1,5},{5,1},{9,13},{13,9},{2,6},{6,2},{1... | collective-permute-start | bytes 786440 | tf_op jit(solution)/shard_map/ppermute | solution.py:16
  18.6 11.2 %collective-permute-start.9 = (f32[256,256]{1,0:T(8,128)S(1)}, f32[256,256]{1,0:T(8,128)S(1)}, u32[]{:S(2)}, u32[]{:S(2)}) collective-permute-start(f32[256,256]{1,0:T(8,128)S(1)} %fusion.18), channel_id=1, source_target_pairs={{0,1},{1,3},{2,0},{3,2},{4,5},{5,7},{6,4},{7,6},{8,9},{9,11},{10,8... | collective-permute-start | bytes 786440 | tf_op jit(solution)/shard_map/ppermute | solution.py:54
  22.0 11.5 %collective-permute-start.10 = (f32[256,256]{1,0:T(8,128)S(1)}, f32[256,256]{1,0:T(8,128)S(1)}, u32[]{:S(2)}, u32[]{:S(2)}) collective-permute-start(f32[256,256]{1,0:T(8,128)S(1)} %fusion.22), channel_id=1, source_target_pairs={{0,1},{1,3},{2,0},{3,2},{4,5},{5,7},{6,4},{7,6},{8,9},{9,11},{10,8... | collective-permute-start | bytes 786440 | tf_op jit(solution)/shard_map/ppermute | solution.py:54
  26.1 18.5 %collective-permute-start.5 = (f32[256,512]{1,0:T(8,128)}, f32[256,512]{1,0:T(8,128)S(1)}, u32[]{:S(2)}, u32[]{:S(2)}) collective-permute-start(f32[256,512]{1,0:T(8,128)} %slice.26), channel_id=1, source_target_pairs={{0,1},{1,0},{2,3},{3,2},{4,5},{5,4},{6,7},{7,6},{8,9},{9,8},{10,11... | collective-permute-start | bytes 1572872 | tf_op jit(solution)/shard_map/ppermute | solution.py:16
  26.6 30.7 %collective-permute-start.8 = (f32[256,512]{1,0:T(8,128)S(1)}, f32[256,512]{1,0:T(8,128)}, u32[]{:S(2)}, u32[]{:S(2)}) collective-permute-start(f32[256,512]{1,0:T(8,128)S(1)} %fusion.11), channel_id=1, source_target_pairs={{0,3},{3,0},{4,7},{7,4},{8,11},{11,8},{12,15},{15,12},{16,19},{19,... | collective-permute-start | bytes 1572872 | tf_op jit(solution)/shard_map/ppermute | solution.py:101
  34.4 22.9 %collective-permute-start.11 = (f32[256,512]{1,0:T(8,128)}, f32[256,512]{1,0:T(8,128)}, u32[]{:S(2)}, u32[]{:S(2)}) collective-permute-start(f32[256,512]{1,0:T(8,128)} %add.79), channel_id=1, source_target_pairs={{1,2},{2,1},{5,6},{6,5},{9,10},{10,9},{13,14},{14,13},{17,18},{18,... | collective-permute-start | bytes 1572872 | tf_op jit(solution)/shard_map/ppermute | solution.py:105
  35.9 0.7 copy-start.2
  58.7 3.6 %collective-permute-start.12 = (f32[1,512]{1,0:T(1,128)S(1)}, f32[1,512]{1,0:T(1,128)S(1)}, u32[]{:S(2)}, u32[]{:S(2)}) collective-permute-start(f32[1,512]{1,0:T(1,128)S(1)} %bitcast.2), channel_id=1, source_target_pairs={{0,16},{16,0},{1,17},{17,1},{2,18},{18,2},{3,19},{19,3},{4,20},{20... | collective-permute-start | bytes 6152 | tf_op jit(solution)/shard_map/ppermute | solution.py:16
  62.4 5.7 %collective-permute-start.13 = (f32[1,512]{1,0:T(1,128)S(1)}, f32[1,512]{1,0:T(1,128)S(1)}, u32[]{:S(2)}, u32[]{:S(2)}) collective-permute-start(f32[1,512]{1,0:T(1,128)S(1)} %add.87), channel_id=1, source_target_pairs={{0,1},{1,0},{2,3},{3,2},{4,5},{5,4},{6,7},{7,6},{8,9},{9,8},{10,11... | collective-permute-start | bytes 6152 | tf_op jit(solution)/shard_map/ppermute | solution.py:16
  68.1 4.5 %collective-permute-start.14 = (f32[1,512]{1,0:T(1,128)S(1)}, f32[1,512]{1,0:T(1,128)S(1)}, u32[]{:S(2)}, u32[]{:S(2)}) collective-permute-start(f32[1,512]{1,0:T(1,128)S(1)} %add.88), channel_id=1, source_target_pairs={{0,2},{1,3},{2,0},{3,1},{4,6},{5,7},{6,4},{7,5},{8,10},{9,11},{10,... | collective-permute-start | bytes 6152 | tf_op jit(solution)/shard_map/ppermute | solution.py:16

commit v2 on v1

--- a/solution.py
+++ b/solution.py
@@ -26,13 +26,11 @@
     return pieces
 
 
-def in_order(pieces, axis, dim):
-    index = lax.axis_index(axis)
-    blocks = [pieces[j] for j in range(len(pieces))]
-    for bit in bits_of(len(pieces)):
-        flip = (index & bit) != 0
+def flipped(blocks, mask):
+    for bit in bits_of(len(blocks)):
+        flip = (mask & bit) != 0
         blocks = [jnp.where(flip, blocks[j ^ bit], blocks[j]) for j in range(len(blocks))]
-    return jnp.concatenate(blocks, axis=dim)
+    return blocks
 
 
 def total_over(value, axis):
@@ -76,16 +74,37 @@
         for j in list(pieces):
             pieces[j ^ 1] = swap(pieces[j], "col", 1)
         pieces.update({0: mine, 1: blocks_of(lax.optimization_barrier(near), offsets)})
-        return in_order(lax.optimization_barrier(pieces), "col", 1)
+        return pieces
+
+    def left_blocks(pieces, count, *earlier):
+        pieces, _ = lax.optimization_barrier((pieces, earlier))
+        return [
+            jnp.concatenate([pieces[j][k * own:(k + 1) * own] for j in range(len(pieces))], axis=1)
+            for k in range(count)
+        ]
+
+    shared = lax.axis_size("col") // row_count
+    mask = (row ^ (col // shared)) * shared + col % shared
 
     def gather_right(value):
         pieces = far_pieces(value, "row", 0)
         pieces[0] = value
-        return in_order(pieces, "row", 0)
+        depth = value.shape[0] // shared
+        blocks = [
+            pieces[i][k * depth:(k + 1) * depth] for i in range(row_count) for k in range(shared)
+        ]
+        return jnp.concatenate(flipped(blocks, mask), axis=0)
 
-    first = gather_left((2, 3))
-    rest = gather_left((1, 0))
-    rights = [gather_right(lax.optimization_barrier(regularizer[:, h * part:(h + 1) * part])) for h in range(2)]
+    first, second, rest = (
+        gather_left(offsets)
+        for offsets in ((2,), (3,), (1, 0))
+    )
+    halves = [lax.optimization_barrier(regularizer[:, h * part:(h + 1) * part]) for h in range(2)]
+    rights = [gather_right(halves[h]) for h in range(2)]
+    ahead_right = gather_right(swap(halves[1], "layer", 1))
+    ahead = swap(blocks_of(flow_matrix, (1,)), "layer", 1)
+    ahead = far_pieces(ahead, "col", 1) | {0: ahead}
+    ahead.update({j ^ 1: swap(ahead[j], "col", 1) for j in list(ahead)})
 
     def product(left, right):
         value = jnp.dot(
@@ -95,15 +114,29 @@
 
     kept = kept_tiles(pattern, row * rows + layer * own, own, col * width, width, tile)
     relay = (1, last, 0, last - 1)
-    right = jnp.concatenate(rights, axis=1)
-    seconds = [exchange(product(first[:own], rights[h]), relay) for h in range(2)]
-    third = product(first[own:], right)
-    across = lax.ppermute(third, "layer", [(0, last), (last, 0)])
-    others = product(rest, right)
-    beside = swap(others[:own], "layer", 1)
-    seconds = jnp.concatenate(seconds, axis=1)
-    passed = lax.ppermute(third + seconds, "layer", [(1, 2), (2, 1)])
-    expanded = others[own:] + beside + across + passed + jnp.where(end, seconds, 0.0)
+    inward = [(0, 1), (last, last - 1)]
+    (first,) = left_blocks(first, 1)
+    heads = [product(first, rights[h]) for h in range(2)]
+    (second,) = left_blocks(second, 1, heads[0])
+    thirds = [product(second, rights[h]) for h in range(2)]
+    rest, _ = lax.optimization_barrier((rest, thirds[0]))
+    rest = jnp.concatenate([rest[j] for j in range(len(rest))], axis=1)
+    fourth = product(rest, rights[0])
+    mine = product(rest[own:], rights[1])
+    ahead, kept = lax.optimization_barrier((ahead, kept, fourth))[:2]
+    (ahead,) = left_blocks(ahead, 1)
+    mine = mine + product(ahead, ahead_right)
+    hop_1 = exchange(heads[0], relay)
+    hop_2 = lax.ppermute(thirds[1], "layer", inward)
+    hop_3 = exchange(heads[1] + hop_2, relay)
+    hop_4 = swap(thirds[0] + jnp.where(end, 0.0, hop_1), "layer", last)
+    hop_5 = swap(fourth[:own], "layer", 1)
+    hop_6 = lax.ppermute(thirds[1] + hop_3, "layer", [(1, 2), (2, 1)])
+    results = [
+        fourth[own:] + hop_5 + hop_4 + jnp.where(end, hop_1, 0.0),
+        mine + hop_6 + jnp.where(end, hop_3, 0.0),
+    ]
+    expanded = jnp.concatenate(results, axis=1)
     pruned = expanded * kept
     squared = pruned * pruned
     totals = jnp.sum(squared, axis=0, keepdims=True)

time: 73.7 us -> 87.1 us (1.18)
  starting transfers between devices: 23.8 us -> 33.5 us
  waiting for transfers between devices: 40.2 us -> 45.2 us
  other arithmetic: 3.65 us -> 2.41 us
    ppermute x11 -> x20, starting transfers between devices: 14.6 us -> 25.3 us  [swap(): lax.ppermute(value, axis, [(i, i ^ bit) for i in range(lax.axis_size(axis...]
    ppermute x11 -> x20, waiting for transfers between devices: 24 us -> 33.9 us  [swap(): lax.ppermute(value, axis, [(i, i ^ bit) for i in range(lax.axis_size(axis...]
    ppermute x2, waiting for transfers between devices: 12.6 us -> 5.74 us  [the longest x1 5.74 us: shards(): hop_2 = lax.ppermute(thirds[1], 'layer', inward)]
    ppermute x2, waiting for transfers between devices: 3.63 us -> 5.53 us  [exchange(): return lax.ppermute(value, 'layer', list(enumerate(targets)))]
    ppermute x2, starting transfers between devices: 4.47 us -> 3.04 us  [exchange(): return lax.ppermute(value, 'layer', list(enumerate(targets)))]
    reduce_sum x1, other arithmetic: 1.46 us -> 0.1 us  [shards(): totals = jnp.sum(squared, axis=0, keepdims=True)]
    dynamic_slice x2, local copies, waits for them, and re-layouts: 1.18 us -> 0.08 us  [blocks_of(): lax.dynamic_slice_in_dim(values, (layer ^ k) * own, own, 0)]
    slice x1, local copies, waits for them, and re-layouts: 0.04 us -> 1.12 us  [shards(): regularizer[:, h * part:(h + 1) * part]]
  transfers between devices with their start and end apart: 15 -> 24, of which waited for: 9 -> 11; matrix products, arithmetic and copies ran while one was open for 6% -> 6% of each run, Pallas kernels for 0% -> 0%
where the time goes in v2:
time: 87.1 us; the launch traced here: 86.9 us
  waiting for transfers between devices  45.2 us (52%)
  starting transfers between devices  33.5 us (38%)
  matrix products  3.32 us (4%)
  other arithmetic  2.41 us (3%)
  local copies, waits for them, and re-layouts  2.08 us (2%)
    ppermute x20, waiting for transfers between devices, swap(): lax.ppermute(value, axis, [(i, i ^ bit) for i in range(lax.axis_size(axis...  33.9 us
    ppermute x20, starting transfers between devices, swap(): lax.ppermute(value, axis, [(i, i ^ bit) for i in range(lax.axis_size(axis...  25.3 us
    ppermute x1, waiting for transfers between devices, shards(): hop_2 = lax.ppermute(thirds[1], 'layer', inward)  5.74 us
    ppermute x2, waiting for transfers between devices, exchange(): return lax.ppermute(value, 'layer', list(enumerate(targets)))  5.53 us
    ppermute x1, starting transfers between devices, shards(): hop_2 = lax.ppermute(thirds[1], 'layer', inward)  4.51 us
    ppermute x2, starting transfers between devices, exchange(): return lax.ppermute(value, 'layer', list(enumerate(targets)))  3.04 us
    dot_general x7, matrix products, product(): jnp.dot(left, right, precision=lax.Precision.HIGH, preferred_element_type...  2.94 us
  transfers between devices with their start and end apart: 24, of which 11 were waited for; matrix products, arithmetic and copies ran while one was open for 6% of the time, Pallas kernels for 0%

profile of v2, /device:TPU:0, one launch (start us, length us, event | category | flops | bytes accessed | tf_op | source)
XLA Modules:
  0.0 86.9 jit_solution(4876586341152946423)
XLA Ops:
  0.0 1.1 %fusion.44 = (f32[256,256]{1,0:T(8,128)S(1)}, f32[256,256]{1,0:T(8,128)S(1)}) fusion(f32[256,512]{1,0:T(8,128)} %param.4), kind=kLoop, calls=%fused_computation.106 | loop fusion | bytes 1048576 | tf_op jit(solution)/shard_map/slice | solution.py:102
  1.1 3.1 %collective-permute-start.16 = (f32[256,256]{1,0:T(8,128)S(1)}, f32[256,256]{1,0:T(8,128)S(1)}, u32[]{:S(2)}, u32[]{:S(2)}) collective-permute-start(f32[256,256]{1,0:T(8,128)S(1)} %get-tuple-element.55), channel_id=1, source_target_pairs={{0,1},{1,0},{2,3},{3,2},{4,5},{5,4},{6,7},{7,6},{8,9},{9,8},{10,11... | collective-permute-start | bytes 786440 | tf_op jit(solution)/shard_map/ppermute | solution.py:16
  4.2 1.5 %collective-permute-start.11 = (f32[256,256]{1,0:T(8,128)S(1)}, f32[256,256]{1,0:T(8,128)S(1)}, u32[]{:S(2)}, u32[]{:S(2)}) collective-permute-start(f32[256,256]{1,0:T(8,128)S(1)} %get-tuple-element.55), channel_id=1, source_target_pairs={{0,16},{16,0},{1,17},{17,1},{2,18},{18,2},{3,19},{19,3},{4,20},{20... | collective-permute-start | bytes 786440 | tf_op jit(solution)/shard_map/ppermute | solution.py:16
  5.7 0.5 collective-permute-start.7
  6.5 0.7 copy-done.1
  7.6 10.1 %collective-permute-done.7 = f32[256,256]{1,0:T(8,128)} collective-permute-done((f32[256,256]{1,0:T(8,128)S(1)}, f32[256,256]{1,0:T(8,128)}, u32[]{:S(2)}, u32[]{:S(2)}) %collective-permute-start.7) | collective-permute-done | bytes 262176 | tf_op jit(solution)/shard_map/ppermute | solution.py:16
  17.7 1.5 %collective-permute-start.5 = (f32[256,128]{1,0:T(8,128)S(1)}, f32[256,128]{1,0:T(8,128)S(1)}, u32[]{:S(2)}, u32[]{:S(2)}) collective-permute-start(f32[256,128]{1,0:T(8,128)S(1)} %get-tuple-element.26), channel_id=1, source_target_pairs={{0,8},{4,12},{8,0},{12,4},{1,9},{5,13},{9,1},{13,5},{2,10},{6,14},... | collective-permute-start | bytes 393224 | tf_op jit(solution)/shard_map/ppermute | solution.py:16
  19.3 1.0 %broadcast_select_fusion.11 = (f32[128,256]{1,0:T(8,128)S(1)}, f32[128,256]{1,0:T(8,128)S(1)}, f32[128,256]{1,0:T(8,128)S(1)}, f32[128,256]{1,0:T(8,128)S(1)}) fusion(pred[]{:T(512)S(6)} %ne.68, f32[256,256]{1,0:T(8,128)S(1)} %get-tuple-element.56, f32[256,256]{1,0:T(8,128)} %collective-permute-done.7, pred[]{:T(512)S(6)} %ne.69), kind=kLoop, calls=%fused_computation.62 | loop fusion | flops 262144 | bytes 1048578 | tf_op jit(solution)/shard_map/jit(_where)/select_n | solution.py:32
  20.3 2.4 %collective-permute-done.5 = f32[256,128]{1,0:T(8,128)S(1)} collective-permute-done((f32[256,128]{1,0:T(8,128)S(1)}, f32[256,128]{1,0:T(8,128)S(1)}, u32[]{:S(2)}, u32[]{:S(2)}) %collective-permute-start.5) | collective-permute-done | bytes 131104 | tf_op jit(solution)/shard_map/ppermute | solution.py:16
  22.7 1.5 %collective-permute-start.3 = (f32[256,128]{1,0:T(8,128)S(1)}, f32[256,128]{1,0:T(8,128)S(1)}, u32[]{:S(2)}, u32[]{:S(2)}) collective-permute-start(f32[256,128]{1,0:T(8,128)S(1)} %get-tuple-element.30), channel_id=1, source_target_pairs={{0,8},{4,12},{8,0},{12,4},{1,9},{5,13},{9,1},{13,5},{2,10},{6,14},... | collective-permute-start | bytes 393224 | tf_op jit(solution)/shard_map/ppermute | solution.py:16
  24.2 0.5 collective-permute-start.1
  24.7 1.6 %collective-permute-start.14 = (f32[256,128]{1,0:T(8,128)S(1)}, f32[256,128]{1,0:T(8,128)S(1)}, u32[]{:S(2)}, u32[]{:S(2)}) collective-permute-start(f32[256,128]{1,0:T(8,128)S(1)} %collective-permute-done.12), channel_id=1, source_target_pairs={{0,8},{4,12},{8,0},{12,4},{1,9},{5,13},{9,1},{13,5},{2,10},{6,14},... | collective-permute-start | bytes 393224 | tf_op jit(solution)/shard_map/ppermute | solution.py:16
  26.4 2.6 %collective-permute-done.3 = f32[256,128]{1,0:T(8,128)S(1)} collective-permute-done((f32[256,128]{1,0:T(8,128)S(1)}, f32[256,128]{1,0:T(8,128)S(1)}, u32[]{:S(2)}, u32[]{:S(2)}) %collective-permute-start.3) | collective-permute-done | bytes 131104 | tf_op jit(solution)/shard_map/ppermute | solution.py:16
  29.1 0.5 collective-permute-start.4
  29.6 3.1 %collective-permute-done.1 = f32[512,128]{1,0:T(8,128)S(1)} collective-permute-done((f32[512,128]{1,0:T(8,128)S(1)}, f32[512,128]{1,0:T(8,128)S(1)}, u32[]{:S(2)}, u32[]{:S(2)}) %collective-permute-start.1) | collective-permute-done | bytes 262176 | tf_op jit(solution)/shard_map/ppermute | solution.py:16
  32.7 1.4 %collective-permute-done.14 = f32[256,128]{1,0:T(8,128)S(1)} collective-permute-done((f32[256,128]{1,0:T(8,128)S(1)}, f32[256,128]{1,0:T(8,128)S(1)}, u32[]{:S(2)}, u32[]{:S(2)}) %collective-permute-start.14) | collective-permute-done | bytes 131104 | tf_op jit(solution)/shard_map/ppermute | solution.py:16
  34.1 1.5 %collective-permute-start.17 = (f32[256,256]{1,0:T(8,128)S(1)}, f32[256,256]{1,0:T(8,128)S(1)}, u32[]{:S(2)}, u32[]{:S(2)}) collective-permute-start(f32[256,256]{1,0:T(8,128)S(1)} %collective-permute-done.16), channel_id=1, source_target_pairs={{0,16},{16,0},{1,17},{17,1},{2,18},{18,2},{3,19},{19,3},{4,20},{20... | collective-permute-start | bytes 786440 | tf_op jit(solution)/shard_map/ppermute | solution.py:16
  37.2 0.6 fusion.26
  38.2 4.5 %collective-permute-start.18 = (f32[256,256]{1,0:T(8,128)S(1)}, f32[256,256]{1,0:T(8,128)S(1)}, u32[]{:S(2)}, u32[]{:S(2)}) collective-permute-start(f32[256,256]{1,0:T(8,128)S(1)} %fusion.25), channel_id=1, source_target_pairs={{0,1},{3,2},{4,5},{7,6},{8,9},{11,10},{12,13},{15,14},{16,17},{19,... | collective-permute-start | bytes 786440 | tf_op jit(solution)/shard_map/ppermute | solution.py:130
  43.7 5.7 %collective-permute-done.18 = f32[256,256]{1,0:T(8,128)S(1)} collective-permute-done((f32[256,256]{1,0:T(8,128)S(1)}, f32[256,256]{1,0:T(8,128)S(1)}, u32[]{:S(2)}, u32[]{:S(2)}) %collective-permute-start.18) | collective-permute-done | bytes 262176 | tf_op jit(solution)/shard_map/ppermute | solution.py:130
  49.4 2.5 %collective-permute-start.19 = (f32[256,256]{1,0:T(8,128)S(1)}, f32[256,256]{1,0:T(8,128)S(1)}, u32[]{:S(2)}, u32[]{:S(2)}) collective-permute-start(f32[256,256]{1,0:T(8,128)S(1)} %add.110), channel_id=1, source_target_pairs={{0,1},{1,3},{2,0},{3,2},{4,5},{5,7},{6,4},{7,6},{8,9},{9,11},{10,8... | collective-permute-start | bytes 786440 | tf_op jit(solution)/shard_map/ppermute | solution.py:52
  52.0 3.2 %collective-permute-start.10 = (f32[256,256]{1,0:T(8,128)S(1)}, f32[256,256]{1,0:T(8,128)S(1)}, u32[]{:S(2)}, u32[]{:S(2)}) collective-permute-start(f32[256,256]{1,0:T(8,128)S(1)} %select_add_fusion.1), channel_id=1, source_target_pairs={{0,3},{1,2},{2,1},{3,0},{4,7},{5,6},{6,5},{7,4},{8,11},{9,10},{10,... | collective-permute-start | bytes 786440 | tf_op jit(solution)/shard_map/ppermute | solution.py:16
  55.2 5.5 %collective-permute-done.19 = f32[256,256]{1,0:T(8,128)S(1)} collective-permute-done((f32[256,256]{1,0:T(8,128)S(1)}, f32[256,256]{1,0:T(8,128)S(1)}, u32[]{:S(2)}, u32[]{:S(2)}) %collective-permute-start.19) | collective-permute-done | bytes 262176 | tf_op jit(solution)/shard_map/ppermute | solution.py:52
  60.8 0.7 collective-permute-start.20
  61.9 7.3 %collective-permute-done.10 = f32[256,256]{1,0:T(8,128)S(1)} collective-permute-done((f32[256,256]{1,0:T(8,128)S(1)}, f32[256,256]{1,0:T(8,128)S(1)}, u32[]{:S(2)}, u32[]{:S(2)}) %collective-permute-start.10) | collective-permute-done | bytes 262176 | tf_op jit(solution)/shard_map/ppermute | solution.py:16
  69.4 0.6 collective-permute-start.21
  70.0 3.0 %collective-permute-done.21 = f32[1,512]{1,0:T(1,128)S(1)} collective-permute-done((f32[1,512]{1,0:T(1,128)S(1)}, f32[1,512]{1,0:T(1,128)S(1)}, u32[]{:S(2)}, u32[]{:S(2)}) %collective-permute-start.21) | collective-permute-done | bytes 2080 | tf_op jit(solution)/shard_map/ppermute | solution.py:16
  73.1 6.9 %collective-permute-start.22 = (f32[1,512]{1,0:T(1,128)S(1)}, f32[1,512]{1,0:T(1,128)S(1)}, u32[]{:S(2)}, u32[]{:S(2)}) collective-permute-start(f32[1,512]{1,0:T(1,128)S(1)} %add.114), channel_id=1, source_target_pairs={{0,1},{1,0},{2,3},{3,2},{4,5},{5,4},{6,7},{7,6},{8,9},{9,8},{10,11... | collective-permute-start | bytes 6152 | tf_op jit(solution)/shard_map/ppermute | solution.py:16
  79.9 1.6 %collective-permute-done.22 = f32[1,512]{1,0:T(1,128)S(1)} collective-permute-done((f32[1,512]{1,0:T(1,128)S(1)}, f32[1,512]{1,0:T(1,128)S(1)}, u32[]{:S(2)}, u32[]{:S(2)}) %collective-permute-start.22) | collective-permute-done | bytes 2080 | tf_op jit(solution)/shard_map/ppermute | solution.py:16
  81.5 2.2 %collective-permute-start.23 = (f32[1,512]{1,0:T(1,128)S(1)}, f32[1,512]{1,0:T(1,128)S(1)}, u32[]{:S(2)}, u32[]{:S(2)}) collective-permute-start(f32[1,512]{1,0:T(1,128)S(1)} %add.115), channel_id=1, source_target_pairs={{0,2},{1,3},{2,0},{3,1},{4,6},{5,7},{6,4},{7,5},{8,10},{9,11},{10,... | collective-permute-start | bytes 6152 | tf_op jit(solution)/shard_map/ppermute | solution.py:16
  83.7 2.3 %collective-permute-done.23 = f32[1,512]{1,0:T(1,128)S(1)} collective-permute-done((f32[1,512]{1,0:T(1,128)S(1)}, f32[1,512]{1,0:T(1,128)S(1)}, u32[]{:S(2)}, u32[]{:S(2)}) %collective-permute-start.23) | collective-permute-done | bytes 2080 | tf_op jit(solution)/shard_map/ppermute | solution.py:16
  86.0 0.9 %divide_multiply_fusion = f32[256,512]{1,0:T(8,128)} fusion(f32[512]{0:T(512)S(1)} %bitcast.9, f32[256,512]{1,0:T(8,128)S(1)} %fusion, f32[256,256]{1,0:T(8,128)S(1)} %select_add_fusion, f32[256,256]{1,0:T(8,128)S(1)} %fusion.22), kind=kLoop, calls=%fused_computation.23 | loop fusion | flops 655360 | bytes 1574912 | tf_op jit(solution)/shard_map/mul | solution.py:144
  (61 shorter events, 4.3 us)
Async XLA Ops:
  0.0 5.7 %copy-start = (f32[1024,128]{1,0:T(8,128)S(1)}, f32[1024,128]{1,0:T(8,128)}, u32[]{:S(2)}) copy-start(f32[1024,128]{1,0:T(8,128)} %param.3) | copy-start | bytes 1572868
  1.1 33.0 %collective-permute-start.16 = (f32[256,256]{1,0:T(8,128)S(1)}, f32[256,256]{1,0:T(8,128)S(1)}, u32[]{:S(2)}, u32[]{:S(2)}) collective-permute-start(f32[256,256]{1,0:T(8,128)S(1)} %get-tuple-element.55), channel_id=1, source_target_pairs={{0,1},{1,0},{2,3},{3,2},{4,5},{5,4},{6,7},{7,6},{8,9},{9,8},{10,11... | collective-permute-start | bytes 786440 | tf_op jit(solution)/shard_map/ppermute | solution.py:16
  4.2 20.5 %collective-permute-start.11 = (f32[256,256]{1,0:T(8,128)S(1)}, f32[256,256]{1,0:T(8,128)S(1)}, u32[]{:S(2)}, u32[]{:S(2)}) collective-permute-start(f32[256,256]{1,0:T(8,128)S(1)} %get-tuple-element.55), channel_id=1, source_target_pairs={{0,16},{16,0},{1,17},{17,1},{2,18},{18,2},{3,19},{19,3},{4,20},{20... | collective-permute-start | bytes 786440 | tf_op jit(solution)/shard_map/ppermute | solution.py:16
  5.7 19.0 %collective-permute-start = (f32[1024,128]{1,0:T(8,128)S(1)}, f32[1024,128]{1,0:T(8,128)S(1)}, u32[]{:S(2)}, u32[]{:S(2)}) collective-permute-start(f32[1024,128]{1,0:T(8,128)S(1)} %copy-done), channel_id=1, source_target_pairs={{0,4},{4,0},{8,12},{12,8},{1,5},{5,1},{9,13},{13,9},{2,6},{6,2},{1... | collective-permute-start | bytes 1572872 | tf_op jit(solution)/shard_map/ppermute | solution.py:16
  5.7 12.0 %collective-permute-start.7 = (f32[256,256]{1,0:T(8,128)S(1)}, f32[256,256]{1,0:T(8,128)}, u32[]{:S(2)}, u32[]{:S(2)}) collective-permute-start(f32[256,256]{1,0:T(8,128)S(1)} %get-tuple-element.56), channel_id=1, source_target_pairs={{0,16},{16,0},{1,17},{17,1},{2,18},{18,2},{3,19},{19,3},{4,20},{20... | collective-permute-start | bytes 786440 | tf_op jit(solution)/shard_map/ppermute | solution.py:16
  6.3 17.9 %collective-permute-start.12 = (f32[256,128]{1,0:T(8,128)S(1)}, f32[256,128]{1,0:T(8,128)S(1)}, u32[]{:S(2)}, u32[]{:S(2)}) collective-permute-start(f32[256,128]{1,0:T(8,128)S(1)} %get-tuple-element.67), channel_id=1, source_target_pairs={{0,1},{1,0},{2,3},{3,2},{4,5},{5,4},{6,7},{7,6},{8,9},{9,8},{10,11... | collective-permute-start | bytes 393224 | tf_op jit(solution)/shard_map/ppermute | solution.py:16
  6.5 0.7 copy-start.1
  17.7 5.0 %collective-permute-start.5 = (f32[256,128]{1,0:T(8,128)S(1)}, f32[256,128]{1,0:T(8,128)S(1)}, u32[]{:S(2)}, u32[]{:S(2)}) collective-permute-start(f32[256,128]{1,0:T(8,128)S(1)} %get-tuple-element.26), channel_id=1, source_target_pairs={{0,8},{4,12},{8,0},{12,4},{1,9},{5,13},{9,1},{13,5},{2,10},{6,14},... | collective-permute-start | bytes 393224 | tf_op jit(solution)/shard_map/ppermute | solution.py:16
  22.7 6.4 %collective-permute-start.3 = (f32[256,128]{1,0:T(8,128)S(1)}, f32[256,128]{1,0:T(8,128)S(1)}, u32[]{:S(2)}, u32[]{:S(2)}) collective-permute-start(f32[256,128]{1,0:T(8,128)S(1)} %get-tuple-element.30), channel_id=1, source_target_pairs={{0,8},{4,12},{8,0},{12,4},{1,9},{5,13},{9,1},{13,5},{2,10},{6,14},... | collective-permute-start | bytes 393224 | tf_op jit(solution)/shard_map/ppermute | solution.py:16
  24.2 8.5 %collective-permute-start.1 = (f32[512,128]{1,0:T(8,128)S(1)}, f32[512,128]{1,0:T(8,128)S(1)}, u32[]{:S(2)}, u32[]{:S(2)}) collective-permute-start(f32[512,128]{1,0:T(8,128)S(1)} %pad_maximum_fusion.2), channel_id=1, source_target_pairs={{0,8},{4,12},{8,0},{12,4},{1,9},{5,13},{9,1},{13,5},{2,10},{6,14},... | collective-permute-start | bytes 786440 | tf_op jit(solution)/shard_map/ppermute | solution.py:16
  24.7 4.3 %collective-permute-start.6 = (f32[256,128]{1,0:T(8,128)S(1)}, f32[256,128]{1,0:T(8,128)S(1)}, u32[]{:S(2)}, u32[]{:S(2)}) collective-permute-start(f32[256,128]{1,0:T(8,128)S(1)} %collective-permute-done.5), channel_id=1, source_target_pairs={{0,4},{4,0},{8,12},{12,8},{1,5},{5,1},{9,13},{13,9},{2,6},{6,2},{1... | collective-permute-start | bytes 393224 | tf_op jit(solution)/shard_map/ppermute | solution.py:16
  24.7 9.3 %collective-permute-start.14 = (f32[256,128]{1,0:T(8,128)S(1)}, f32[256,128]{1,0:T(8,128)S(1)}, u32[]{:S(2)}, u32[]{:S(2)}) collective-permute-start(f32[256,128]{1,0:T(8,128)S(1)} %collective-permute-done.12), channel_id=1, source_target_pairs={{0,8},{4,12},{8,0},{12,4},{1,9},{5,13},{9,1},{13,5},{2,10},{6,14},... | collective-permute-start | bytes 393224 | tf_op jit(solution)/shard_map/ppermute | solution.py:16
  29.1 14.5 %collective-permute-start.13 = (f32[256,128]{1,0:T(8,128)S(1)}, f32[256,128]{1,0:T(8,128)S(1)}, u32[]{:S(2)}, u32[]{:S(2)}) collective-permute-start(f32[256,128]{1,0:T(8,128)S(1)} %collective-permute-done.12), channel_id=1, source_target_pairs={{0,4},{4,0},{8,12},{12,8},{1,5},{5,1},{9,13},{13,9},{2,6},{6,2},{1... | collective-permute-start | bytes 393224 | tf_op jit(solution)/shard_map/ppermute | solution.py:16
  29.1 7.0 %collective-permute-start.4 = (f32[256,128]{1,0:T(8,128)S(1)}, f32[256,128]{1,0:T(8,128)S(1)}, u32[]{:S(2)}, u32[]{:S(2)}) collective-permute-start(f32[256,128]{1,0:T(8,128)S(1)} %collective-permute-done.3), channel_id=1, source_target_pairs={{0,4},{4,0},{8,12},{12,8},{1,5},{5,1},{9,13},{13,9},{2,6},{6,2},{1... | collective-permute-start | bytes 393224 | tf_op jit(solution)/shard_map/ppermute | solution.py:16
  32.7 4.4 %collective-permute-start.2 = (f32[512,128]{1,0:T(8,128)S(1)}, f32[512,128]{1,0:T(8,128)S(1)}, u32[]{:S(2)}, u32[]{:S(2)}) collective-permute-start(f32[512,128]{1,0:T(8,128)S(1)} %collective-permute-done.1), channel_id=1, source_target_pairs={{0,4},{4,0},{8,12},{12,8},{1,5},{5,1},{9,13},{13,9},{2,6},{6,2},{1... | collective-permute-start | bytes 786440 | tf_op jit(solution)/shard_map/ppermute | solution.py:16
  34.1 9.6 %collective-permute-start.15 = (f32[256,128]{1,0:T(8,128)S(1)}, f32[256,128]{1,0:T(8,128)S(1)}, u32[]{:S(2)}, u32[]{:S(2)}) collective-permute-start(f32[256,128]{1,0:T(8,128)S(1)} %collective-permute-done.14), channel_id=1, source_target_pairs={{0,4},{4,0},{8,12},{12,8},{1,5},{5,1},{9,13},{13,9},{2,6},{6,2},{1... | collective-permute-start | bytes 393224 | tf_op jit(solution)/shard_map/ppermute | solution.py:16
  34.1 21.1 %collective-permute-start.17 = (f32[256,256]{1,0:T(8,128)S(1)}, f32[256,256]{1,0:T(8,128)S(1)}, u32[]{:S(2)}, u32[]{:S(2)}) collective-permute-start(f32[256,256]{1,0:T(8,128)S(1)} %collective-permute-done.16), channel_id=1, source_target_pairs={{0,16},{16,0},{1,17},{17,1},{2,18},{18,2},{3,19},{19,3},{4,20},{20... | collective-permute-start | bytes 786440 | tf_op jit(solution)/shard_map/ppermute | solution.py:16
  36.1 15.9 %collective-permute-start.9 = (f32[256,256]{1,0:T(8,128)S(1)}, f32[256,256]{1,0:T(8,128)S(1)}, u32[]{:S(2)}, u32[]{:S(2)}) collective-permute-start(f32[256,256]{1,0:T(8,128)S(1)} %fusion.28), channel_id=1, source_target_pairs={{0,1},{1,3},{2,0},{3,2},{4,5},{5,7},{6,4},{7,6},{8,9},{9,11},{10,8... | collective-permute-start | bytes 786440 | tf_op jit(solution)/shard_map/ppermute | solution.py:52
  38.2 11.2 %collective-permute-start.18 = (f32[256,256]{1,0:T(8,128)S(1)}, f32[256,256]{1,0:T(8,128)S(1)}, u32[]{:S(2)}, u32[]{:S(2)}) collective-permute-start(f32[256,256]{1,0:T(8,128)S(1)} %fusion.25), channel_id=1, source_target_pairs={{0,1},{3,2},{4,5},{7,6},{8,9},{11,10},{12,13},{15,14},{16,17},{19,... | collective-permute-start | bytes 786440 | tf_op jit(solution)/shard_map/ppermute | solution.py:130
  43.6 18.3 %collective-permute-start.8 = (f32[256,256]{1,0:T(8,128)S(1)}, f32[256,256]{1,0:T(8,128)S(1)}, u32[]{:S(2)}, u32[]{:S(2)}) collective-permute-start(f32[256,256]{1,0:T(8,128)S(1)} %slice.73), channel_id=1, source_target_pairs={{0,1},{1,0},{2,3},{3,2},{4,5},{5,4},{6,7},{7,6},{8,9},{9,8},{10,11... | collective-permute-start | bytes 786440 | tf_op jit(solution)/shard_map/ppermute | solution.py:16
  49.4 11.3 %collective-permute-start.19 = (f32[256,256]{1,0:T(8,128)S(1)}, f32[256,256]{1,0:T(8,128)S(1)}, u32[]{:S(2)}, u32[]{:S(2)}) collective-permute-start(f32[256,256]{1,0:T(8,128)S(1)} %add.110), channel_id=1, source_target_pairs={{0,1},{1,3},{2,0},{3,2},{4,5},{5,7},{6,4},{7,6},{8,9},{9,11},{10,8... | collective-permute-start | bytes 786440 | tf_op jit(solution)/shard_map/ppermute | solution.py:52
  52.0 17.1 %collective-permute-start.10 = (f32[256,256]{1,0:T(8,128)S(1)}, f32[256,256]{1,0:T(8,128)S(1)}, u32[]{:S(2)}, u32[]{:S(2)}) collective-permute-start(f32[256,256]{1,0:T(8,128)S(1)} %select_add_fusion.1), channel_id=1, source_target_pairs={{0,3},{1,2},{2,1},{3,0},{4,7},{5,6},{6,5},{7,4},{8,11},{9,10},{10,... | collective-permute-start | bytes 786440 | tf_op jit(solution)/shard_map/ppermute | solution.py:16
  60.8 8.4 %collective-permute-start.20 = (f32[256,256]{1,0:T(8,128)S(1)}, f32[256,256]{1,0:T(8,128)S(1)}, u32[]{:S(2)}, u32[]{:S(2)}) collective-permute-start(f32[256,256]{1,0:T(8,128)S(1)} %add.111), channel_id=1, source_target_pairs={{1,2},{2,1},{5,6},{6,5},{9,10},{10,9},{13,14},{14,13},{17,18},{18,... | collective-permute-start | bytes 786440 | tf_op jit(solution)/shard_map/ppermute | solution.py:134
  69.4 3.6 %collective-permute-start.21 = (f32[1,512]{1,0:T(1,128)S(1)}, f32[1,512]{1,0:T(1,128)S(1)}, u32[]{:S(2)}, u32[]{:S(2)}) collective-permute-start(f32[1,512]{1,0:T(1,128)S(1)} %bitcast.7), channel_id=1, source_target_pairs={{0,16},{16,0},{1,17},{17,1},{2,18},{18,2},{3,19},{19,3},{4,20},{20... | collective-permute-start | bytes 6152 | tf_op jit(solution)/shard_map/ppermute | solution.py:16
  73.1 8.4 %collective-permute-start.22 = (f32[1,512]{1,0:T(1,128)S(1)}, f32[1,512]{1,0:T(1,128)S(1)}, u32[]{:S(2)}, u32[]{:S(2)}) collective-permute-start(f32[1,512]{1,0:T(1,128)S(1)} %add.114), channel_id=1, source_target_pairs={{0,1},{1,0},{2,3},{3,2},{4,5},{5,4},{6,7},{7,6},{8,9},{9,8},{10,11... | collective-permute-start | bytes 6152 | tf_op jit(solution)/shard_map/ppermute | solution.py:16
  81.5 4.5 %collective-permute-start.23 = (f32[1,512]{1,0:T(1,128)S(1)}, f32[1,512]{1,0:T(1,128)S(1)}, u32[]{:S(2)}, u32[]{:S(2)}) collective-permute-start(f32[1,512]{1,0:T(1,128)S(1)} %add.115), channel_id=1, source_target_pairs={{0,2},{1,3},{2,0},{3,1},{4,6},{5,7},{6,4},{7,5},{8,10},{9,11},{10,... | collective-permute-start | bytes 6152 | tf_op jit(solution)/shard_map/ppermute | solution.py:16

commit v3 on v2

--- a/solution.py
+++ b/solution.py
@@ -34,7 +34,8 @@
 
 
 def total_over(value, axis):
-    for bit in bits_of(lax.axis_size(axis))[::-1]:
+    count = lax.axis_size(axis)
+    for bit in [count - 1] + bits_of(count)[1:]:
         value = value + swap(value, axis, bit)
     return value
 
@@ -112,9 +113,11 @@
         )
         return lax.optimization_barrier(value)
 
-    kept = kept_tiles(pattern, row * rows + layer * own, own, col * width, width, tile)
+    kept_rows = own if tile % own else 1
+    kept = kept_tiles(pattern, row * rows + layer * own, kept_rows, col * width, width, tile)
     relay = (1, last, 0, last - 1)
     inward = [(0, 1), (last, last - 1)]
+    middle, outward = [(1, 2), (2, 1)], [(1, last), (2, 0)]
     (first,) = left_blocks(first, 1)
     heads = [product(first, rights[h]) for h in range(2)]
     (second,) = left_blocks(second, 1, heads[0])
@@ -128,13 +131,14 @@
     mine = mine + product(ahead, ahead_right)
     hop_1 = exchange(heads[0], relay)
     hop_2 = lax.ppermute(thirds[1], "layer", inward)
-    hop_3 = exchange(heads[1] + hop_2, relay)
+    hop_3 = lax.ppermute(heads[1], "layer", inward)
     hop_4 = swap(thirds[0] + jnp.where(end, 0.0, hop_1), "layer", last)
     hop_5 = swap(fourth[:own], "layer", 1)
-    hop_6 = lax.ppermute(thirds[1] + hop_3, "layer", [(1, 2), (2, 1)])
+    hop_6 = lax.ppermute(thirds[1] + hop_3, "layer", middle)
+    hop_7 = lax.ppermute(heads[1] + hop_2, "layer", outward)
     results = [
         fourth[own:] + hop_5 + hop_4 + jnp.where(end, hop_1, 0.0),
-        mine + hop_6 + jnp.where(end, hop_3, 0.0),
+        mine + hop_6 + hop_7,
     ]
     expanded = jnp.concatenate(results, axis=1)
     pruned = expanded * kept

time: 87.1 us -> 77.3 us (0.89)
  waiting for transfers between devices: 45.2 us -> 38.1 us
  starting transfers between devices: 33.5 us -> 31.8 us
  other arithmetic: 2.41 us -> 1.42 us
    ppermute x2 -> x1, waiting for transfers between devices: 5.53 us -> 0.01 us  [exchange(): return lax.ppermute(value, 'layer', list(enumerate(targets)))]
    ppermute x1 -> x3, waiting for transfers between devices: 0.01 us -> 4.28 us  [the longest x1 4.28 us: shards(): hop_3 = lax.ppermute(heads[1], 'layer', inward)]
    ppermute x1, waiting for transfers between devices: 5.74 us -> 2.06 us  [shards(): hop_2 = lax.ppermute(thirds[1], 'layer', inward)]
    ppermute x20, starting transfers between devices: 25.3 us -> 22.4 us  [swap(): lax.ppermute(value, axis, [(i, i ^ bit) for i in range(lax.axis_size(axis...]
    ppermute x1 -> x3, starting transfers between devices: 0.68 us -> 3.28 us  [the longest x1 1.31 us: shards(): hop_3 = lax.ppermute(heads[1], 'layer', inward)]
    ppermute x20, waiting for transfers between devices: 33.9 us -> 31.8 us  [swap(): lax.ppermute(value, axis, [(i, i ^ bit) for i in range(lax.axis_size(axis...]
    ppermute x2 -> x1, starting transfers between devices: 3.04 us -> 1.63 us  [exchange(): return lax.ppermute(value, 'layer', list(enumerate(targets)))]
    select_n x3, other arithmetic: 1.11 us -> 0.14 us  [flipped(): jnp.where(flip, blocks[j ^ bit], blocks[j])]
  transfers between devices with their start and end apart: 24 -> 25, of which waited for: 11 -> 12; matrix products, arithmetic and copies ran while one was open for 6% -> 5% of each run, Pallas kernels for 0% -> 0%
where the time goes in v3:
time: 77.3 us; the launch traced here: 77 us
  waiting for transfers between devices  38.1 us (49%)
  starting transfers between devices  31.8 us (41%)
  matrix products  3.15 us (4%)
  local copies, waits for them, and re-layouts  2.1 us (3%)
  other arithmetic  1.42 us (2%)
    ppermute x20, waiting for transfers between devices, swap(): lax.ppermute(value, axis, [(i, i ^ bit) for i in range(lax.axis_size(axis...  31.8 us
    ppermute x20, starting transfers between devices, swap(): lax.ppermute(value, axis, [(i, i ^ bit) for i in range(lax.axis_size(axis...  22.4 us
    ppermute x1, starting transfers between devices, shards(): hop_2 = lax.ppermute(thirds[1], 'layer', inward)  4.52 us
    ppermute x1, waiting for transfers between devices, shards(): hop_3 = lax.ppermute(heads[1], 'layer', inward)  4.28 us
    dot_general x7, matrix products, product(): jnp.dot(left, right, precision=lax.Precision.HIGH, preferred_element_type...  2.92 us
    ppermute x1, waiting for transfers between devices, shards(): hop_2 = lax.ppermute(thirds[1], 'layer', inward)  2.06 us
    ppermute x1, starting transfers between devices, exchange(): return lax.ppermute(value, 'layer', list(enumerate(targets)))  1.63 us
  transfers between devices with their start and end apart: 25, of which 12 were waited for; matrix products, arithmetic and copies ran while one was open for 5% of the time, Pallas kernels for 0%

profile of v3, /device:TPU:0, one launch (start us, length us, event | category | flops | bytes accessed | tf_op | source)
XLA Modules:
  0.0 77.0 jit_solution(11881498303984907846)
XLA Ops:
  0.0 1.1 %fusion.48 = (f32[256,256]{1,0:T(8,128)S(1)}, f32[256,256]{1,0:T(8,128)S(1)}) fusion(f32[256,512]{1,0:T(8,128)} %param.4), kind=kLoop, calls=%fused_computation.104 | loop fusion | bytes 1048576 | tf_op jit(solution)/shard_map/slice | solution.py:103
  1.1 3.0 %collective-permute-start.11 = (f32[256,256]{1,0:T(8,128)S(1)}, f32[256,256]{1,0:T(8,128)S(1)}, u32[]{:S(2)}, u32[]{:S(2)}) collective-permute-start(f32[256,256]{1,0:T(8,128)S(1)} %get-tuple-element.64), channel_id=1, source_target_pairs={{0,16},{16,0},{1,17},{17,1},{2,18},{18,2},{3,19},{19,3},{4,20},{20... | collective-permute-start | bytes 786440 | tf_op jit(solution)/shard_map/ppermute | solution.py:16
  4.2 1.6 %collective-permute-start.16 = (f32[256,256]{1,0:T(8,128)S(1)}, f32[256,256]{1,0:T(8,128)S(1)}, u32[]{:S(2)}, u32[]{:S(2)}) collective-permute-start(f32[256,256]{1,0:T(8,128)S(1)} %get-tuple-element.64), channel_id=1, source_target_pairs={{0,1},{1,0},{2,3},{3,2},{4,5},{5,4},{6,7},{7,6},{8,9},{9,8},{10,11... | collective-permute-start | bytes 786440 | tf_op jit(solution)/shard_map/ppermute | solution.py:16
  5.7 0.5 collective-permute-start.7
  6.5 0.7 copy-done.1
  7.5 3.9 %collective-permute-done.11 = f32[256,256]{1,0:T(8,128)S(1)} collective-permute-done((f32[256,256]{1,0:T(8,128)S(1)}, f32[256,256]{1,0:T(8,128)S(1)}, u32[]{:S(2)}, u32[]{:S(2)}) %collective-permute-start.11) | collective-permute-done | bytes 262176 | tf_op jit(solution)/shard_map/ppermute | solution.py:16
  11.3 2.0 %collective-permute-start.5 = (f32[256,128]{1,0:T(8,128)S(1)}, f32[256,128]{1,0:T(8,128)S(1)}, u32[]{:S(2)}, u32[]{:S(2)}) collective-permute-start(f32[256,128]{1,0:T(8,128)S(1)} %get-tuple-element.26), channel_id=1, source_target_pairs={{0,8},{4,12},{8,0},{12,4},{1,9},{5,13},{9,1},{13,5},{2,10},{6,14},... | collective-permute-start | bytes 393224 | tf_op jit(solution)/shard_map/ppermute | solution.py:16
  13.4 2.9 %collective-permute-done.5 = f32[256,128]{1,0:T(8,128)S(1)} collective-permute-done((f32[256,128]{1,0:T(8,128)S(1)}, f32[256,128]{1,0:T(8,128)S(1)}, u32[]{:S(2)}, u32[]{:S(2)}) %collective-permute-start.5) | collective-permute-done | bytes 131104 | tf_op jit(solution)/shard_map/ppermute | solution.py:16
  16.3 2.4 %collective-permute-start.3 = (f32[256,128]{1,0:T(8,128)S(1)}, f32[256,128]{1,0:T(8,128)S(1)}, u32[]{:S(2)}, u32[]{:S(2)}) collective-permute-start(f32[256,128]{1,0:T(8,128)S(1)} %get-tuple-element.30), channel_id=1, source_target_pairs={{0,8},{4,12},{8,0},{12,4},{1,9},{5,13},{9,1},{13,5},{2,10},{6,14},... | collective-permute-start | bytes 393224 | tf_op jit(solution)/shard_map/ppermute | solution.py:16
  18.8 2.0 %collective-permute-start.14 = (f32[256,128]{1,0:T(8,128)S(1)}, f32[256,128]{1,0:T(8,128)S(1)}, u32[]{:S(2)}, u32[]{:S(2)}) collective-permute-start(f32[256,128]{1,0:T(8,128)S(1)} %collective-permute-done.12), channel_id=1, source_target_pairs={{0,8},{4,12},{8,0},{12,4},{1,9},{5,13},{9,1},{13,5},{2,10},{6,14},... | collective-permute-start | bytes 393224 | tf_op jit(solution)/shard_map/ppermute | solution.py:16
  21.0 1.1 %collective-permute-done.3 = f32[256,128]{1,0:T(8,128)S(1)} collective-permute-done((f32[256,128]{1,0:T(8,128)S(1)}, f32[256,128]{1,0:T(8,128)S(1)}, u32[]{:S(2)}, u32[]{:S(2)}) %collective-permute-start.3) | collective-permute-done | bytes 131104 | tf_op jit(solution)/shard_map/ppermute | solution.py:16
  22.6 3.8 %collective-permute-done.1 = f32[512,128]{1,0:T(8,128)S(1)} collective-permute-done((f32[512,128]{1,0:T(8,128)S(1)}, f32[512,128]{1,0:T(8,128)S(1)}, u32[]{:S(2)}, u32[]{:S(2)}) %collective-permute-start.1) | collective-permute-done | bytes 262176 | tf_op jit(solution)/shard_map/ppermute | solution.py:16
  26.4 1.4 %collective-permute-done.14 = f32[256,128]{1,0:T(8,128)S(1)} collective-permute-done((f32[256,128]{1,0:T(8,128)S(1)}, f32[256,128]{1,0:T(8,128)S(1)}, u32[]{:S(2)}, u32[]{:S(2)}) %collective-permute-start.14) | collective-permute-done | bytes 131104 | tf_op jit(solution)/shard_map/ppermute | solution.py:16
  27.8 1.8 %collective-permute-start.17 = (f32[256,256]{1,0:T(8,128)S(1)}, f32[256,256]{1,0:T(8,128)S(1)}, u32[]{:S(2)}, u32[]{:S(2)}) collective-permute-start(f32[256,256]{1,0:T(8,128)S(1)} %collective-permute-done.16), channel_id=1, source_target_pairs={{0,16},{16,0},{1,17},{17,1},{2,18},{18,2},{3,19},{19,3},{4,20},{20... | collective-permute-start | bytes 786440 | tf_op jit(solution)/shard_map/ppermute | solution.py:16
  30.0 1.6 %collective-permute-start.9 = (f32[256,256]{1,0:T(8,128)S(1)}, f32[256,256]{1,0:T(8,128)S(1)}, u32[]{:S(2)}, u32[]{:S(2)}) collective-permute-start(f32[256,256]{1,0:T(8,128)S(1)} %fusion.26), channel_id=1, source_target_pairs={{0,1},{1,3},{2,0},{3,2},{4,5},{5,7},{6,4},{7,6},{8,9},{9,11},{10,8... | collective-permute-start | bytes 786440 | tf_op jit(solution)/shard_map/ppermute | solution.py:53
  32.3 0.6 fusion.24
  34.1 4.5 %collective-permute-start.20 = (f32[256,256]{1,0:T(8,128)S(1)}, f32[256,256]{1,0:T(8,128)S(1)}, u32[]{:S(2)}, u32[]{:S(2)}) collective-permute-start(f32[256,256]{1,0:T(8,128)S(1)} %fusion.23), channel_id=1, source_target_pairs={{0,1},{3,2},{4,5},{7,6},{8,9},{11,10},{12,13},{15,14},{16,17},{19,... | collective-permute-start | bytes 786440 | tf_op jit(solution)/shard_map/ppermute | solution.py:133
  38.7 1.3 %collective-permute-start.18 = (f32[256,256]{1,0:T(8,128)S(1)}, f32[256,256]{1,0:T(8,128)S(1)}, u32[]{:S(2)}, u32[]{:S(2)}) collective-permute-start(f32[256,256]{1,0:T(8,128)S(1)} %fusion.22), channel_id=1, source_target_pairs={{0,1},{3,2},{4,5},{7,6},{8,9},{11,10},{12,13},{15,14},{16,17},{19,... | collective-permute-start | bytes 786440 | tf_op jit(solution)/shard_map/ppermute | solution.py:134
  40.1 3.1 %collective-permute-start.10 = (f32[256,256]{1,0:T(8,128)S(1)}, f32[256,256]{1,0:T(8,128)S(1)}, u32[]{:S(2)}, u32[]{:S(2)}) collective-permute-start(f32[256,256]{1,0:T(8,128)S(1)} %select_add_fusion), channel_id=1, source_target_pairs={{0,3},{1,2},{2,1},{3,0},{4,7},{5,6},{6,5},{7,4},{8,11},{9,10},{10,... | collective-permute-start | bytes 786440 | tf_op jit(solution)/shard_map/ppermute | solution.py:16
  43.2 2.1 %collective-permute-done.20 = f32[256,256]{1,0:T(8,128)S(1)} collective-permute-done((f32[256,256]{1,0:T(8,128)S(1)}, f32[256,256]{1,0:T(8,128)S(1)}, u32[]{:S(2)}, u32[]{:S(2)}) %collective-permute-start.20) | collective-permute-done | bytes 262176 | tf_op jit(solution)/shard_map/ppermute | solution.py:133
  45.3 1.3 %collective-permute-start.21 = (f32[256,256]{1,0:T(8,128)S(1)}, f32[256,256]{1,0:T(8,128)S(1)}, u32[]{:S(2)}, u32[]{:S(2)}) collective-permute-start(f32[256,256]{1,0:T(8,128)S(1)} %add.100), channel_id=1, source_target_pairs={{1,3},{2,0},{5,7},{6,4},{9,11},{10,8},{13,15},{14,12},{17,19},{18,... | collective-permute-start | bytes 786440 | tf_op jit(solution)/shard_map/ppermute | solution.py:138
  46.6 4.3 %collective-permute-done.18 = f32[256,256]{1,0:T(8,128)S(1)} collective-permute-done((f32[256,256]{1,0:T(8,128)S(1)}, f32[256,256]{1,0:T(8,128)S(1)}, u32[]{:S(2)}, u32[]{:S(2)}) %collective-permute-start.18) | collective-permute-done | bytes 262176 | tf_op jit(solution)/shard_map/ppermute | solution.py:134
  50.9 0.7 collective-permute-start.19
  52.0 4.5 %collective-permute-done.8 = f32[256,256]{1,0:T(8,128)S(1)} collective-permute-done((f32[256,256]{1,0:T(8,128)S(1)}, f32[256,256]{1,0:T(8,128)S(1)}, u32[]{:S(2)}, u32[]{:S(2)}) %collective-permute-start.8) | collective-permute-done | bytes 262176 | tf_op jit(solution)/shard_map/ppermute | solution.py:16
  56.5 6.6 %collective-permute-done.10 = f32[256,256]{1,0:T(8,128)S(1)} collective-permute-done((f32[256,256]{1,0:T(8,128)S(1)}, f32[256,256]{1,0:T(8,128)S(1)}, u32[]{:S(2)}, u32[]{:S(2)}) %collective-permute-start.10) | collective-permute-done | bytes 262176 | tf_op jit(solution)/shard_map/ppermute | solution.py:16
  63.4 0.6 collective-permute-start.22
  64.0 3.0 %collective-permute-done.22 = f32[1,512]{1,0:T(1,128)S(1)} collective-permute-done((f32[1,512]{1,0:T(1,128)S(1)}, f32[1,512]{1,0:T(1,128)S(1)}, u32[]{:S(2)}, u32[]{:S(2)}) %collective-permute-start.22) | collective-permute-done | bytes 2080 | tf_op jit(solution)/shard_map/ppermute | solution.py:16
  67.0 2.4 %collective-permute-start.23 = (f32[1,512]{1,0:T(1,128)S(1)}, f32[1,512]{1,0:T(1,128)S(1)}, u32[]{:S(2)}, u32[]{:S(2)}) collective-permute-start(f32[1,512]{1,0:T(1,128)S(1)} %add.102), channel_id=1, source_target_pairs={{0,3},{1,2},{2,1},{3,0},{4,7},{5,6},{6,5},{7,4},{8,11},{9,10},{10,... | collective-permute-start | bytes 6152 | tf_op jit(solution)/shard_map/ppermute | solution.py:16
  69.4 3.0 %collective-permute-done.23 = f32[1,512]{1,0:T(1,128)S(1)} collective-permute-done((f32[1,512]{1,0:T(1,128)S(1)}, f32[1,512]{1,0:T(1,128)S(1)}, u32[]{:S(2)}, u32[]{:S(2)}) %collective-permute-start.23) | collective-permute-done | bytes 2080 | tf_op jit(solution)/shard_map/ppermute | solution.py:16
  72.4 2.2 %collective-permute-start.24 = (f32[1,512]{1,0:T(1,128)S(1)}, f32[1,512]{1,0:T(1,128)S(1)}, u32[]{:S(2)}, u32[]{:S(2)}) collective-permute-start(f32[1,512]{1,0:T(1,128)S(1)} %add.103), channel_id=1, source_target_pairs={{0,1},{1,0},{2,3},{3,2},{4,5},{5,4},{6,7},{7,6},{8,9},{9,8},{10,11... | collective-permute-start | bytes 6152 | tf_op jit(solution)/shard_map/ppermute | solution.py:16
  74.6 1.6 %collective-permute-done.24 = f32[1,512]{1,0:T(1,128)S(1)} collective-permute-done((f32[1,512]{1,0:T(1,128)S(1)}, f32[1,512]{1,0:T(1,128)S(1)}, u32[]{:S(2)}, u32[]{:S(2)}) %collective-permute-start.24) | collective-permute-done | bytes 2080 | tf_op jit(solution)/shard_map/ppermute | solution.py:16
  76.2 0.9 %divide_multiply_fusion = f32[256,512]{1,0:T(8,128)} fusion(f32[256,256]{1,0:T(8,128)S(1)} %add_add_fusion, f32[256,256]{1,0:T(8,128)S(1)} %fusion.21, f32[512]{0:T(512)S(1)} %bitcast.24, f32[512]{0:T(512)S(1)} %bitcast.21), kind=kLoop, calls=%fused_computation.23 | loop fusion | flops 655360 | bytes 1052672 | tf_op jit(solution)/shard_map/mul | solution.py:148
  (62 shorter events, 4.2 us)
Async XLA Ops:
  0.0 5.7 %copy-start = (f32[1024,128]{1,0:T(8,128)S(1)}, f32[1024,128]{1,0:T(8,128)}, u32[]{:S(2)}) copy-start(f32[1024,128]{1,0:T(8,128)} %param.3) | copy-start | bytes 1572868
  1.1 10.2 %collective-permute-start.11 = (f32[256,256]{1,0:T(8,128)S(1)}, f32[256,256]{1,0:T(8,128)S(1)}, u32[]{:S(2)}, u32[]{:S(2)}) collective-permute-start(f32[256,256]{1,0:T(8,128)S(1)} %get-tuple-element.64), channel_id=1, source_target_pairs={{0,16},{16,0},{1,17},{17,1},{2,18},{18,2},{3,19},{19,3},{4,20},{20... | collective-permute-start | bytes 786440 | tf_op jit(solution)/shard_map/ppermute | solution.py:16
  4.2 23.6 %collective-permute-start.16 = (f32[256,256]{1,0:T(8,128)S(1)}, f32[256,256]{1,0:T(8,128)S(1)}, u32[]{:S(2)}, u32[]{:S(2)}) collective-permute-start(f32[256,256]{1,0:T(8,128)S(1)} %get-tuple-element.64), channel_id=1, source_target_pairs={{0,1},{1,0},{2,3},{3,2},{4,5},{5,4},{6,7},{7,6},{8,9},{9,8},{10,11... | collective-permute-start | bytes 786440 | tf_op jit(solution)/shard_map/ppermute | solution.py:16
  5.7 13.1 %collective-permute-start = (f32[1024,128]{1,0:T(8,128)S(1)}, f32[1024,128]{1,0:T(8,128)S(1)}, u32[]{:S(2)}, u32[]{:S(2)}) collective-permute-start(f32[1024,128]{1,0:T(8,128)S(1)} %copy-done), channel_id=1, source_target_pairs={{0,4},{4,0},{8,12},{12,8},{1,5},{5,1},{9,13},{13,9},{2,6},{6,2},{1... | collective-permute-start | bytes 1572872 | tf_op jit(solution)/shard_map/ppermute | solution.py:16
  5.7 13.0 %collective-permute-start.7 = (f32[256,256]{1,0:T(8,128)S(1)}, f32[256,256]{1,0:T(8,128)S(1)}, u32[]{:S(2)}, u32[]{:S(2)}) collective-permute-start(f32[256,256]{1,0:T(8,128)S(1)} %get-tuple-element.63), channel_id=1, source_target_pairs={{0,16},{16,0},{1,17},{17,1},{2,18},{18,2},{3,19},{19,3},{4,20},{20... | collective-permute-start | bytes 786440 | tf_op jit(solution)/shard_map/ppermute | solution.py:16
  6.3 12.4 %collective-permute-start.12 = (f32[256,128]{1,0:T(8,128)S(1)}, f32[256,128]{1,0:T(8,128)S(1)}, u32[]{:S(2)}, u32[]{:S(2)}) collective-permute-start(f32[256,128]{1,0:T(8,128)S(1)} %get-tuple-element.55), channel_id=1, source_target_pairs={{0,1},{1,0},{2,3},{3,2},{4,5},{5,4},{6,7},{7,6},{8,9},{9,8},{10,11... | collective-permute-start | bytes 393224 | tf_op jit(solution)/shard_map/ppermute | solution.py:16
  6.5 0.7 copy-start.1
  11.3 5.0 %collective-permute-start.5 = (f32[256,128]{1,0:T(8,128)S(1)}, f32[256,128]{1,0:T(8,128)S(1)}, u32[]{:S(2)}, u32[]{:S(2)}) collective-permute-start(f32[256,128]{1,0:T(8,128)S(1)} %get-tuple-element.26), channel_id=1, source_target_pairs={{0,8},{4,12},{8,0},{12,4},{1,9},{5,13},{9,1},{13,5},{2,10},{6,14},... | collective-permute-start | bytes 393224 | tf_op jit(solution)/shard_map/ppermute | solution.py:16
  16.3 5.7 %collective-permute-start.3 = (f32[256,128]{1,0:T(8,128)S(1)}, f32[256,128]{1,0:T(8,128)S(1)}, u32[]{:S(2)}, u32[]{:S(2)}) collective-permute-start(f32[256,128]{1,0:T(8,128)S(1)} %get-tuple-element.30), channel_id=1, source_target_pairs={{0,8},{4,12},{8,0},{12,4},{1,9},{5,13},{9,1},{13,5},{2,10},{6,14},... | collective-permute-start | bytes 393224 | tf_op jit(solution)/shard_map/ppermute | solution.py:16
  18.7 7.6 %collective-permute-start.1 = (f32[512,128]{1,0:T(8,128)S(1)}, f32[512,128]{1,0:T(8,128)S(1)}, u32[]{:S(2)}, u32[]{:S(2)}) collective-permute-start(f32[512,128]{1,0:T(8,128)S(1)} %pad_maximum_fusion.2), channel_id=1, source_target_pairs={{0,8},{4,12},{8,0},{12,4},{1,9},{5,13},{9,1},{13,5},{2,10},{6,14},... | collective-permute-start | bytes 786440 | tf_op jit(solution)/shard_map/ppermute | solution.py:16
  18.8 3.3 %collective-permute-start.6 = (f32[256,128]{1,0:T(8,128)S(1)}, f32[256,128]{1,0:T(8,128)S(1)}, u32[]{:S(2)}, u32[]{:S(2)}) collective-permute-start(f32[256,128]{1,0:T(8,128)S(1)} %collective-permute-done.5), channel_id=1, source_target_pairs={{0,4},{4,0},{8,12},{12,8},{1,5},{5,1},{9,13},{13,9},{2,6},{6,2},{1... | collective-permute-start | bytes 393224 | tf_op jit(solution)/shard_map/ppermute | solution.py:16
  18.8 8.9 %collective-permute-start.14 = (f32[256,128]{1,0:T(8,128)S(1)}, f32[256,128]{1,0:T(8,128)S(1)}, u32[]{:S(2)}, u32[]{:S(2)}) collective-permute-start(f32[256,128]{1,0:T(8,128)S(1)} %collective-permute-done.12), channel_id=1, source_target_pairs={{0,8},{4,12},{8,0},{12,4},{1,9},{5,13},{9,1},{13,5},{2,10},{6,14},... | collective-permute-start | bytes 393224 | tf_op jit(solution)/shard_map/ppermute | solution.py:16
  22.1 16.6 %collective-permute-start.13 = (f32[256,128]{1,0:T(8,128)S(1)}, f32[256,128]{1,0:T(8,128)S(1)}, u32[]{:S(2)}, u32[]{:S(2)}) collective-permute-start(f32[256,128]{1,0:T(8,128)S(1)} %collective-permute-done.12), channel_id=1, source_target_pairs={{0,4},{4,0},{8,12},{12,8},{1,5},{5,1},{9,13},{13,9},{2,6},{6,2},{1... | collective-permute-start | bytes 393224 | tf_op jit(solution)/shard_map/ppermute | solution.py:16
  22.1 8.0 %collective-permute-start.4 = (f32[256,128]{1,0:T(8,128)S(1)}, f32[256,128]{1,0:T(8,128)S(1)}, u32[]{:S(2)}, u32[]{:S(2)}) collective-permute-start(f32[256,128]{1,0:T(8,128)S(1)} %collective-permute-done.3), channel_id=1, source_target_pairs={{0,4},{4,0},{8,12},{12,8},{1,5},{5,1},{9,13},{13,9},{2,6},{6,2},{1... | collective-permute-start | bytes 393224 | tf_op jit(solution)/shard_map/ppermute | solution.py:16
  26.4 5.8 %collective-permute-start.2 = (f32[512,128]{1,0:T(8,128)S(1)}, f32[512,128]{1,0:T(8,128)S(1)}, u32[]{:S(2)}, u32[]{:S(2)}) collective-permute-start(f32[512,128]{1,0:T(8,128)S(1)} %collective-permute-done.1), channel_id=1, source_target_pairs={{0,4},{4,0},{8,12},{12,8},{1,5},{5,1},{9,13},{13,9},{2,6},{6,2},{1... | collective-permute-start | bytes 786440 | tf_op jit(solution)/shard_map/ppermute | solution.py:16
  27.8 12.2 %collective-permute-start.15 = (f32[256,128]{1,0:T(8,128)S(1)}, f32[256,128]{1,0:T(8,128)S(1)}, u32[]{:S(2)}, u32[]{:S(2)}) collective-permute-start(f32[256,128]{1,0:T(8,128)S(1)} %collective-permute-done.14), channel_id=1, source_target_pairs={{0,4},{4,0},{8,12},{12,8},{1,5},{5,1},{9,13},{13,9},{2,6},{6,2},{1... | collective-permute-start | bytes 393224 | tf_op jit(solution)/shard_map/ppermute | solution.py:16
  27.8 15.4 %collective-permute-start.17 = (f32[256,256]{1,0:T(8,128)S(1)}, f32[256,256]{1,0:T(8,128)S(1)}, u32[]{:S(2)}, u32[]{:S(2)}) collective-permute-start(f32[256,256]{1,0:T(8,128)S(1)} %collective-permute-done.16), channel_id=1, source_target_pairs={{0,16},{16,0},{1,17},{17,1},{2,18},{18,2},{3,19},{19,3},{4,20},{20... | collective-permute-start | bytes 786440 | tf_op jit(solution)/shard_map/ppermute | solution.py:16
  30.0 10.0 %collective-permute-start.9 = (f32[256,256]{1,0:T(8,128)S(1)}, f32[256,256]{1,0:T(8,128)S(1)}, u32[]{:S(2)}, u32[]{:S(2)}) collective-permute-start(f32[256,256]{1,0:T(8,128)S(1)} %fusion.26), channel_id=1, source_target_pairs={{0,1},{1,3},{2,0},{3,2},{4,5},{5,7},{6,4},{7,6},{8,9},{9,11},{10,8... | collective-permute-start | bytes 786440 | tf_op jit(solution)/shard_map/ppermute | solution.py:53
  34.1 11.2 %collective-permute-start.20 = (f32[256,256]{1,0:T(8,128)S(1)}, f32[256,256]{1,0:T(8,128)S(1)}, u32[]{:S(2)}, u32[]{:S(2)}) collective-permute-start(f32[256,256]{1,0:T(8,128)S(1)} %fusion.23), channel_id=1, source_target_pairs={{0,1},{3,2},{4,5},{7,6},{8,9},{11,10},{12,13},{15,14},{16,17},{19,... | collective-permute-start | bytes 786440 | tf_op jit(solution)/shard_map/ppermute | solution.py:133
  38.7 12.2 %collective-permute-start.18 = (f32[256,256]{1,0:T(8,128)S(1)}, f32[256,256]{1,0:T(8,128)S(1)}, u32[]{:S(2)}, u32[]{:S(2)}) collective-permute-start(f32[256,256]{1,0:T(8,128)S(1)} %fusion.22), channel_id=1, source_target_pairs={{0,1},{3,2},{4,5},{7,6},{8,9},{11,10},{12,13},{15,14},{16,17},{19,... | collective-permute-start | bytes 786440 | tf_op jit(solution)/shard_map/ppermute | solution.py:134
  40.0 16.5 %collective-permute-start.8 = (f32[256,256]{1,0:T(8,128)S(1)}, f32[256,256]{1,0:T(8,128)S(1)}, u32[]{:S(2)}, u32[]{:S(2)}) collective-permute-start(f32[256,256]{1,0:T(8,128)S(1)} %slice.73), channel_id=1, source_target_pairs={{0,1},{1,0},{2,3},{3,2},{4,5},{5,4},{6,7},{7,6},{8,9},{9,8},{10,11... | collective-permute-start | bytes 786440 | tf_op jit(solution)/shard_map/ppermute | solution.py:16
  40.1 23.0 %collective-permute-start.10 = (f32[256,256]{1,0:T(8,128)S(1)}, f32[256,256]{1,0:T(8,128)S(1)}, u32[]{:S(2)}, u32[]{:S(2)}) collective-permute-start(f32[256,256]{1,0:T(8,128)S(1)} %select_add_fusion), channel_id=1, source_target_pairs={{0,3},{1,2},{2,1},{3,0},{4,7},{5,6},{6,5},{7,4},{8,11},{9,10},{10,... | collective-permute-start | bytes 786440 | tf_op jit(solution)/shard_map/ppermute | solution.py:16
  45.3 17.9 %collective-permute-start.21 = (f32[256,256]{1,0:T(8,128)S(1)}, f32[256,256]{1,0:T(8,128)S(1)}, u32[]{:S(2)}, u32[]{:S(2)}) collective-permute-start(f32[256,256]{1,0:T(8,128)S(1)} %add.100), channel_id=1, source_target_pairs={{1,3},{2,0},{5,7},{6,4},{9,11},{10,8},{13,15},{14,12},{17,19},{18,... | collective-permute-start | bytes 786440 | tf_op jit(solution)/shard_map/ppermute | solution.py:138
  50.9 12.3 %collective-permute-start.19 = (f32[256,256]{1,0:T(8,128)S(1)}, f32[256,256]{1,0:T(8,128)S(1)}, u32[]{:S(2)}, u32[]{:S(2)}) collective-permute-start(f32[256,256]{1,0:T(8,128)S(1)} %add.98), channel_id=1, source_target_pairs={{1,2},{2,1},{5,6},{6,5},{9,10},{10,9},{13,14},{14,13},{17,18},{18,... | collective-permute-start | bytes 786440 | tf_op jit(solution)/shard_map/ppermute | solution.py:137
  63.4 3.6 %collective-permute-start.22 = (f32[1,512]{1,0:T(1,128)S(1)}, f32[1,512]{1,0:T(1,128)S(1)}, u32[]{:S(2)}, u32[]{:S(2)}) collective-permute-start(f32[1,512]{1,0:T(1,128)S(1)} %bitcast.22), channel_id=1, source_target_pairs={{0,16},{16,0},{1,17},{17,1},{2,18},{18,2},{3,19},{19,3},{4,20},{20... | collective-permute-start | bytes 6152 | tf_op jit(solution)/shard_map/ppermute | solution.py:16
  67.0 5.4 %collective-permute-start.23 = (f32[1,512]{1,0:T(1,128)S(1)}, f32[1,512]{1,0:T(1,128)S(1)}, u32[]{:S(2)}, u32[]{:S(2)}) collective-permute-start(f32[1,512]{1,0:T(1,128)S(1)} %add.102), channel_id=1, source_target_pairs={{0,3},{1,2},{2,1},{3,0},{4,7},{5,6},{6,5},{7,4},{8,11},{9,10},{10,... | collective-permute-start | bytes 6152 | tf_op jit(solution)/shard_map/ppermute | solution.py:16
  72.4 3.7 %collective-permute-start.24 = (f32[1,512]{1,0:T(1,128)S(1)}, f32[1,512]{1,0:T(1,128)S(1)}, u32[]{:S(2)}, u32[]{:S(2)}) collective-permute-start(f32[1,512]{1,0:T(1,128)S(1)} %add.103), channel_id=1, source_target_pairs={{0,1},{1,0},{2,3},{3,2},{4,5},{5,4},{6,7},{7,6},{8,9},{9,8},{10,11... | collective-permute-start | bytes 6152 | tf_op jit(solution)/shard_map/ppermute | solution.py:16
